TPU v7x, 32 devices: a whole 2x2x4 slice. The times are simulated.
32 devices in a mesh: ctx: 8 (over z, x), pipe: 4 (over y, core).
Axes of the slice: x: 2, y: 2, z: 4, core: 2. Of those that a mesh axis runs over, the one named last changes fastest.
Arguments:
- section_out: bfloat16 [4, 1024, 4096], P('pipe', 'ctx'), may hold values from -6 to 6
- stash: bfloat16 [4, 1024, 4096], P('pipe', 'ctx'), may hold values from -6 to 6
- grad_out: bfloat16 [4, 1024, 4096], P('pipe', 'ctx'), may hold values from -6 to 6
- taps: float32 [4, 3, 7, 4096], P('pipe'), may hold values from -2 to 2
- residues: float32 [4, 16, 256], P('pipe'), may hold values from -2 to 2
- decays: float32 [4, 16, 256], P('pipe'), may hold values from 0.0002 to 0.1
- doc_lengths: int32 [2, 24], replicated, may hold values from 1 to 64, 1024 in all within a row
Outputs:
- mixed: bfloat16 [4, 1024, 4096], P('pipe', 'ctx')
- input_grad: bfloat16 [4, 1024, 4096], P('pipe', 'ctx')
- filter_grad: float32 [4, 16, 256], P('pipe')
- tap_grad: float32 [4, 3, 7, 4096], P('pipe')
Inputs may be any that keep to these rules, and one draw needn't show every extreme that they name: `doc_lengths`: each row sums to 1024 and its largest length is exactly 64.
All inputs are finite; a program needn't handle non-finite values.
Results may differ from a plain program's by a relative error of at most 0.001.
Values may be sent and summed in bfloat16 or wider, within the bound.
A program may use at most 256 MiB of HBM per device.

v0:
```python
import jax
import jax.numpy as jnp
from jax import lax
from jax.sharding import PartitionSpec as P

HIGH = lax.Precision.HIGHEST


def from_behind(value, axis, steps):
    count = lax.axis_size(axis)
    initial, last = (max(0, -steps), min(count, count - steps))
    return lax.ppermute(value, axis, [(source, source + steps) for source in range(initial, last)])


def passed_along(array, axis, by):
    count = lax.axis_size(axis)
    return lax.ppermute(array, axis, [(i, (i + by) % count) for i in range(count)])


def doc_table(lengths, first_pos, count):
    starts = jnp.cumsum(lengths) - lengths
    places = first_pos + jnp.arange(count, dtype=jnp.int32)
    return jnp.sum((starts[None, :] <= places[:, None]).astype(jnp.int32), axis=1) - 1


def layout(lengths, base, rows):
    doc_ext = doc_table(lengths, base - 6, rows + 12)
    local_doc = doc_ext[6 : 6 + rows]
    positions = jnp.arange(rows, dtype=jnp.int32)
    is_start = local_doc != doc_ext[5 : 5 + rows]
    first_start = jnp.min(jnp.where(is_start, positions, rows))
    last_start = jnp.max(jnp.where(is_start, positions, -1))
    keep_flag = (first_start == rows).astype(jnp.float32)
    live_front = (positions < first_start).astype(jnp.float32)
    live_back = (positions >= last_start).astype(jnp.float32)
    same_doc = (
        (local_doc[:, None] == local_doc[None, :]) & (positions[:, None] >= positions[None, :])
    ).astype(jnp.float32)
    return (doc_ext, local_doc, keep_flag, live_front, live_back, same_doc)


def featurize(ext_cols, doc_ext, local_doc, taps_here, rows):
    result = jnp.zeros((3, ext_cols.shape[0], rows), jnp.float32)
    for j in range(7):
        window = ext_cols[:, 6 - j : 6 - j + rows]
        valid = (doc_ext[6 - j : 6 - j + rows] == local_doc).astype(jnp.float32)
        result = result + taps_here[:, j][:, :, None] * (window * valid[None, :])[None]
    return result


def link(earlier, later):
    return (earlier[0] * later[0], later[0][:, None, :] * earlier[1] + later[1])


def link_pairs(earlier, later):
    return link((earlier[0], earlier[1]), (later[0], later[1])) + link(
        (earlier[2], earlier[3]), (later[2], later[3])
    )


def nearby(items, link_fn, sign, depth):
    current = items
    for j in range(depth + 1):
        reach = 1 if j == 0 else 2 ** (j - 1)
        moved = from_behind(current, "ctx", sign * reach)
        current = moved if j == 0 else link_fn(moved, current)
    return current


def on_device(section_out, stash, grad_out, taps, residues, decays, doc_lengths):
    incoming = passed_along(section_out, "pipe", 1)[0]
    upstream = passed_along(grad_out, "pipe", -1)[0]
    stashed = stash[0]
    taps_here = taps[0]
    resid = residues[0]
    rates = decays[0]
    rows, width = stashed.shape
    modes, filters = resid.shape
    group = width // filters
    ctx_size = lax.axis_size("ctx")
    base = lax.axis_index("ctx") * rows
    span = rows * ctx_size // 16 // rows + 1
    depth = (span - 1).bit_length()
    doc_new, local_new, keep_new, front_new, back_new, same_new = layout(doc_lengths[0], base, rows)
    doc_old, local_old, keep_old, front_old, back_old, same_old = layout(doc_lengths[1], base, rows)
    rims = from_behind(jnp.stack([incoming[rows - 6 :], stashed[rows - 6 :]]), "ctx", 1)
    ext_new = jnp.concatenate([rims[0], incoming], axis=0).astype(jnp.float32).T
    ext_old = jnp.concatenate([rims[1], stashed], axis=0).astype(jnp.float32).T
    upstream_cols = upstream.astype(jnp.float32).T
    feat_new = featurize(ext_new, doc_new, local_new, taps_here, rows)
    feat_old = featurize(ext_old, doc_old, local_old, taps_here, rows)
    gated_new = (feat_new[1] * feat_new[2]).reshape(filters, group, rows)
    gated_old = (feat_old[1] * feat_old[2]).reshape(filters, group, rows)
    offsets = jnp.arange(rows, dtype=jnp.float32)
    positions = jnp.arange(rows, dtype=jnp.int32)
    kernel = jnp.sum(resid[:, :, None] * jnp.exp(-rates[:, :, None] * offsets), axis=0)
    lag_index = jnp.clip(positions[:, None] - positions[None, :], 0, rows - 1)
    toeplitz = jnp.take(kernel, lag_index, axis=1)
    toep_new = toeplitz * same_new[None]
    toep_old = toeplitz * same_old[None]
    transfer_rate = jnp.exp(-rates * rows)
    to_end = jnp.exp(-rates[:, :, None] * (rows - 1 - offsets))
    from_start = jnp.exp(-rates[:, :, None] * (offsets + 1.0))
    summary_new = jnp.einsum("mfs,fgs->mgf", to_end * back_new, gated_new, precision=HIGH)
    summary_old = jnp.einsum("mfs,fgs->mgf", to_end * back_old, gated_old, precision=HIGH)
    forward_items = (keep_new * transfer_rate, summary_new, keep_old * transfer_rate, summary_old)
    carried = nearby(forward_items, link_pairs, 1, depth)
    state_new = carried[1]
    state_old = carried[3]
    long_new = jnp.einsum("fts,fgs->fgt", toep_new, gated_new, precision=HIGH)
    long_new = long_new + jnp.einsum(
        "mft,mgf->fgt", resid[:, :, None] * from_start * front_new, state_new, precision=HIGH
    )
    mixed = (feat_new[0] * long_new.reshape(width, rows)).T.astype(jnp.bfloat16)
    long_old = jnp.einsum("fts,fgs->fgt", toep_old, gated_old, precision=HIGH)
    long_old = long_old + jnp.einsum(
        "mft,mgf->fgt", resid[:, :, None] * from_start * front_old, state_old, precision=HIGH
    )
    grad_q = upstream_cols * long_old.reshape(width, rows)
    grad_long = (upstream_cols * feat_old[0]).reshape(filters, group, rows)
    from_zero = jnp.exp(-rates[:, :, None] * offsets)
    reverse_summary = jnp.einsum("mft,fgt->mgf", from_zero * front_old, grad_long, precision=HIGH)
    reverse_items = (keep_old * transfer_rate, reverse_summary)
    returned = nearby(reverse_items, link, -1, depth)
    later_state = returned[1]
    to_next = jnp.exp(-rates[:, :, None] * (rows - offsets))
    grad_gated = jnp.einsum("fts,fgt->fgs", toep_old, grad_long, precision=HIGH)
    grad_gated = grad_gated + jnp.einsum(
        "mfs,mgf->fgs", resid[:, :, None] * to_next * back_old, later_state, precision=HIGH
    )
    grad_gated = grad_gated.reshape(width, rows)
    center = float(rows // 2)
    pair_grad = jnp.einsum("fgt,fgs->fts", grad_long, gated_old, precision=HIGH) * same_old[None]
    rising = jnp.exp(rates[:, :, None] * (offsets - center))
    falling = jnp.exp(-rates[:, :, None] * (offsets - center))
    inner_part = jnp.einsum("fts,mfs->mft", pair_grad, rising, precision=HIGH)
    filter_term = jnp.sum(falling * inner_part, axis=2)
    cross_part = jnp.einsum("fgt,mgf->mft", grad_long, state_old, precision=HIGH)
    filter_term = filter_term + jnp.sum(from_start * front_old * cross_part, axis=2)
    grads = jnp.stack([grad_q, grad_gated * feat_old[2], grad_gated * feat_old[1]])
    rim_rows = jnp.swapaxes(grads[:, :, :6], 1, 2)
    rim_grads = jnp.swapaxes(from_behind(rim_rows, "ctx", -1), 1, 2)
    ext_grads = jnp.concatenate([grads, rim_grads], axis=2)
    back_total = jnp.zeros((width, rows), jnp.float32)
    tap_rows = []
    for j in range(7):
        valid_up = (doc_old[6 + j : 6 + j + rows] == local_old).astype(jnp.float32)
        ahead = ext_grads[:, :, j : j + rows]
        back_total = (
            back_total + jnp.sum(taps_here[:, j][:, :, None] * ahead, axis=0) * valid_up[None, :]
        )
        valid_down = (doc_old[6 - j : 6 - j + rows] == local_old).astype(jnp.float32)
        behind = ext_old[:, 6 - j : 6 - j + rows] * valid_down[None, :]
        tap_rows.append(jnp.sum(grads * behind[None], axis=2))
    tap_term = jnp.stack(tap_rows, axis=1)
    summed = lax.psum((filter_term, tap_term), "ctx")
    return (mixed[None], back_total.T.astype(jnp.bfloat16)[None], summed[0][None], summed[1][None])


def solution(mesh):
    in_specs = (
        P("pipe", "ctx", None),
        P("pipe", "ctx", None),
        P("pipe", "ctx", None),
        P("pipe", None, None, None),
        P("pipe", None, None),
        P("pipe", None, None),
        P(),
    )
    out_specs = (
        P("pipe", "ctx", None),
        P("pipe", "ctx", None),
        P("pipe", None, None),
        P("pipe", None, None, None),
    )
    return jax.shard_map(
        on_device, mesh=mesh, in_specs=in_specs, out_specs=out_specs, check_vma=False
    )
```

profile of v0, /device:TPU:0, one launch (start us, length us, event | category | flops | bytes accessed | tf_op | source)
XLA Modules:
  0.0 575.4 jit_solution(938377799281164614)
XLA Ops:
  7.8 2.3 copy.91
  10.1 2.0 collective-permute-start.3
  23.6 1.7 multiply_reduce_fusion.8
  28.0 62.0 %gather_fusion = f32[16384,256]{1,0:T(8,128)} fusion(f32[256,128]{0,1:T(8,128)S(1)} %copy.87, s32[16384]{0:T(1024)S(1)} %fusion.100), kind=kCustom, calls=%fused_computation | custom fusion | bytes 33619968 | tf_op jit(solution)/shard_map/jit(_take)/gather | solution.py:98
  90.0 18.0 %copy.88 = f32[128,128,256]{1,0,2:T(8,128)} copy(f32[128,128,256]{2,1,0:T(8,128)} %bitcast.130) | data formatting | bytes 33554432 | tf_op jit(solution)/shard_map/jit(_take)/gather | solution.py:98
  109.6 4.5 collective-permute-start.1
  116.6 3.6 convert_bitcast_fusion
  120.1 12.0 %fusion.115 = (f32[4096,128]{0,1:T(8,128)}, f32[4096,128]{0,1:T(8,128)}, f32[4096,128]{0,1:T(8,128)}, f32[4096,128]{0,1:T(8,128)}, f32[4096,128]{0,1:T(8,128)}, /*index=5*/f32[4096,128]{0,1:T(8,128)}, f32[4096,128]{0,1:T(8,128)}) fusion(f32[4096,134]{0,1:T(8,128)} %get-tuple-element.94, f32[128]{0:T(128)} %get-tuple-element.82, f32[128]{0:T(128)} %get-tuple-element.83, ...), kind=kLoop, calls=%fused_computation.200 | loop fusion | flops 3145728 | bytes 29363200 | tf_op jit(solution)/shard_map/slice | solution.py:45
  132.1 2.9 copy.84
  135.0 2.9 copy.83
  137.9 2.9 copy.82
  140.8 2.9 copy.81
  143.7 2.9 copy.80
  146.7 2.9 copy.79
  149.6 2.9 copy.78
  152.5 13.8 %multiply_add_fusion.1 = f32[3,4096,128]{2,1,0:T(8,128)S(1)} fusion(f32[4096,128]{1,0:T(8,128)} %copy.84, f32[3,4096]{1,0:T(4,128)S(1)} %get-tuple-element.95, f32[4096,128]{1,0:T(8,128)} %copy.83, f32[3,4096]{1,0:T(4,128)} %get-tuple-element.96, f32[4096,128]{1,0:T(8,128)} %copy.82, f32[3,4096]{1,0:T(4,128)} %get-tuple-element.97, f32[4096,128]{1,0:T(8,128)} %copy.81, ...), kind=kLoop, calls=%fused_computation.49 | loop fusion | flops 20447232 | bytes 21315584 | tf_op jit(solution)/shard_map/add | solution.py:47
  166.6 2.4 copy-done.2
  170.3 5.0 fusion.57
  175.3 3.3 copy.89
  178.5 5.6 collective-permute-start.2
  184.1 6.0 %fusion.114 = (f32[4096,128]{0,1:T(8,128)}, f32[4096,128]{0,1:T(8,128)}, f32[4096,128]{0,1:T(8,128)}, f32[4096,128]{0,1:T(8,128)}, f32[4096,128]{0,1:T(8,128)}, /*index=5*/f32[4096,128]{0,1:T(8,128)}, f32[4096,128]{0,1:T(8,128)}) fusion(f32[4096,134]{0,1:T(8,128)S(1)} %get-tuple-element.93, f32[128]{0:T(128)} %get-tuple-element.73, ...), kind=kLoop, calls=%fused_computation.199 | loop fusion | flops 3145728 | bytes 29363200 | tf_op jit(solution)/shard_map/slice | solution.py:45
  190.1 1.9 copy.97
  192.0 3.6 copy.98
  195.6 2.9 copy.96
  198.6 2.9 copy.95
  201.5 2.9 copy.94
  204.4 2.9 copy.93
  207.3 2.9 copy.92
  210.2 13.7 %multiply_add_fusion = f32[3,4096,128]{2,1,0:T(8,128)S(1)} fusion(f32[4096,128]{1,0:T(8,128)} %copy.98, f32[4096,128]{1,0:T(8,128)S(1)} %copy.97, f32[4096,128]{1,0:T(8,128)} %copy.96, f32[4096,128]{1,0:T(8,128)} %copy.95, f32[4096,128]{1,0:T(8,128)} %copy.94, f32[4096,128]{1,0:T(8,128)} %copy.93, f32[4096,128]{1,0:T(8,128)} %copy.92, ...), kind=kLoop, calls=%fused_computation.48 | loop fusion | flops 20447232 | bytes 21315584 | tf_op jit(solution)/shard_map/add | solution.py:47
  223.9 2.6 copy-done.1
  226.8 5.0 fusion.69
  231.8 3.3 copy.101
  235.1 1.5 collective-permute-start.5
  236.5 29.6 %fusion.4 = f32[256,16,128]{2,1,0:T(8,128)} fusion(f32[256,16,128]{2,1,0:T(8,128)} %bitcast.135, f32[128,128,256]{1,0,2:T(8,128)} %copy.88, f32[128,128]{1,0:T(8,128)S(1)} %copy-done.23, pred[128,128]{1,0:T(8,128)(4,1)S(1)} %fusion.105), kind=kOutput, calls=%fused_computation.5 | convolution fusion | flops 813694976 | bytes 21053440 | tf_op jit(solution)/shard_map/fts,fgs->fgt/dot_general | solution.py:110
  266.1 3.5 copy.102
  269.6 4.7 fusion.39
  274.4 17.8 %fusion.111 = f32[256,16,128]{2,1,0:T(8,128)} fusion(f32[256,16,128]{2,1,0:T(8,128)S(1)} %fusion.39, f32[256,16,128]{2,1,0:T(8,128)S(1)} %bitcast.127, f32[128,128,256]{1,0,2:T(8,128)} %copy.88, f32[128,128]{1,0:T(8,128)S(1)} %fusion.107, pred[128,128]{1,0:T(8,128)(4,1)S(1)} %fusion.105), kind=kOutput, calls=%fused_computation.198 | convolution fusion | flops 814219264 | bytes 23150592 | tf_op jit(solution)/shard_map/fts,fgt->fgs/dot_general | solution.py:127
  292.2 4.2 bitcast_multiply_fusion.3
  296.4 27.6 %fusion.2 = f32[256,16,128]{2,1,0:T(8,128)} fusion(f32[256,16,128]{2,1,0:T(8,128)S(1)} %bitcast.131, f32[128,128,256]{1,0,2:T(8,128)S(1)} %bitcast.125, f32[128,128]{1,0:T(8,128)S(1)} %fusion.107, pred[128,128]{1,0:T(8,128)(4,1)S(1)} %fusion.105), kind=kOutput, calls=%fused_computation.3 | convolution fusion | flops 813694976 | bytes 21053440 | tf_op jit(solution)/shard_map/fts,fgs->fgt/dot_general | solution.py:115
  324.0 29.1 %fusion.118 = f32[256,128,128]{2,1,0:T(8,128)} fusion(f32[256,16,128]{2,1,0:T(8,128)S(1)} %bitcast.128, f32[256,16,128]{2,1,0:T(8,128)S(1)} %bitcast.132), kind=kOutput, calls=%fused_computation.203 | convolution fusion | flops 805306368 | bytes 20971520 | tf_op jit(solution)/shard_map/fgt,fgs->fts/dot_general | solution.py:133
  353.1 4.9 fusion.63
  358.1 3.4 copy.90
  361.5 4.5 fusion.60
  366.0 2.8 fusion.32
  368.7 3.3 copy.99
  372.0 5.3 collective-permute-start.4
  377.2 29.9 %fusion.34 = f32[16,256]{0,1:T(8,128)} fusion(f32[256,128,128]{2,1,0:T(8,128)} %fusion.118, f32[128,128]{1,0:T(8,128)S(1)} %fusion.107, f32[16,256]{0,1:T(8,128)} %copy.105, f32[128]{0:T(128)S(1)} %copy-done.33, f32[16,256]{0,1:T(8,128)S(1)} %copy.86), kind=kOutput, calls=%fused_computation.73 | convolution fusion | flops 811593728 | bytes 16892416 | tf_op jit(solution)/shard_map/fts,mfs->mft/dot_general | solution.py:136
  407.2 2.3 copy.107
  409.4 3.4 copy.106
  412.8 6.5 %fusion.66 = f32[256,16,128]{2,1,0:T(8,128)S(1)} fusion(f32[256,16,128]{2,1,0:T(8,128)} %fusion.2, f32[16,16,256]{1,0,2:T(8,128)} %copy.106, f32[128]{0:T(128)S(1)} %copy-done.31, f32[128]{0:T(128)S(1)} %copy-done.29, f32[16,256]{0,1:T(8,128)S(1)} %copy.86, f32[16,256]{0,1:T(8,128)S(1)} %copy-done.13), kind=kOutput, calls=%fused_computation.106 | convolution fusion | flops 102760448 | bytes 4490240 | tf_op jit(solution)/shard_map/mft,mgf->fgt/dot_general | solution.py:116
  419.6 2.1 copy-done.5
  422.3 16.9 %multiply_reduce_fusion.1 = (f32[3,4096]{1,0:T(4,128)S(1)}, f32[3,4096]{1,0:T(4,128)}, f32[3,4096]{1,0:T(4,128)}, f32[3,4096]{1,0:T(4,128)}, f32[3,4096]{1,0:T(4...) fusion(f32[4096,128]{1,0:T(8,128)S(1)} %copy-done.8, ...), kind=kLoop, calls=%fused_computation.41 | loop fusion | flops 27701248 | bytes 29753344 | tf_op jit(solution)/shard_map/reduce_sum | solution.py:154
  439.2 3.1 slice_bitcast_fusion
  442.3 4.4 copy.103
  446.7 1.6 collective-permute-start.6
  448.4 4.4 fusion.33
  452.8 39.2 %psum.14 = f32[1,16,256]{1,2,0:T(8,128)S(1)} all-reduce(f32[1,16,256]{1,2,0:T(8,128)S(1)} %add_bitcast_fusion), channel_id=1, replica_groups=mesh['ctx'=8,'pipe'=4] {'ctx'}, use_global_device_ids=true, to_apply=%region_18.19 | all-reduce | flops 4096 | bytes 32768 | tf_op jit(solution)/shard_map/psum | solution.py:156
  498.0 4.0 copy.104
  502.1 9.3 %pad_maximum_fusion = f32[3,4096,134]{2,1,0:T(8,128)} fusion(f32[3,4096,6]{2,1,0:T(8,128)} %bitcast.138, f32[1,4096,128]{2,1,0:T(8,128)} %get-tuple-element.37, f32[1,4096,128]{2,1,0:T(8,128)} %get-tuple-element.36, f32[1,4096,128]{2,1,0:T(8,128)S(1)} %copy-done.4), kind=kLoop, calls=%fused_computation.15 | loop fusion | flops 4939776 | bytes 13172736 | tf_op jit(solution)/shard_map/concatenate | solution.py:143
  511.5 30.8 %fusion.29 = (f32[4096,128]{1,0:T(8,128)S(1)}, f32[4096,128]{1,0:T(8,128)S(1)}, f32[4096,128]{1,0:T(8,128)}, f32[4096,128]{1,0:T(8,128)}, f32[4096,128]{1,0:T(8,128)}, /*index=5*/f32[4096,128]{1,0:T(8,128)}) fusion(f32[3,4096,134]{2,1,0:T(8,128)} %pad_maximum_fusion, f32[3,4096]{1,0:T(4,128)S(1)} %copy-done.21, f32[3,4096]{1,0:T(4,128)S(1)} %get-tuple-element.95, ...), kind=kLoop, calls=%fused_computation.37 | loop fusion | flops 15728640 | bytes 50626560 | tf_op jit(solution)/shard_map/reduce_sum | solution.py:150
  542.3 5.5 fusion.98
  547.8 2.3 copy.108
  550.0 16.6 %all-reduce.2.cloned.1.call-done = f32[1,3,7,4096]{3,0,2,1:T(1,128)} async-done(((f32[1,3,7,4096]{3,0,2,1:T(1,128)}), f32[1,3,7,4096]{3,0,2,1:T(1,128)}) %all-reduce.2.cloned.1.call-update) | async-done | bytes 344080 | tf_op jit(solution)/shard_map/psum | solution.py:156
  566.6 1.7 copy.129
  (164 shorter events, 27.6 us)
Async XLA Ops:
  7.2 4.9 copy-start.32
  7.2 11.1 %copy-start.25 = (f32[1,3,7,4096]{3,0,2,1:T(1,128)S(1)}, f32[1,3,7,4096]{3,0,2,1:T(1,128)}, u32[]{:S(2)}) copy-start(f32[1,3,7,4096]{3,0,2,1:T(1,128)} %param.10) | copy-start | bytes 1032196
  7.2 11.6 %copy-start.27 = (f32[1,16,256]{2,1,0:T(8,128)S(1)}, f32[1,16,256]{2,1,0:T(8,128)}, u32[]{:S(2)}) copy-start(f32[1,16,256]{2,1,0:T(8,128)} %param.12) | copy-start | bytes 49156
  7.2 11.7 %copy-start.28 = (f32[1,16,256]{2,1,0:T(8,128)S(1)}, f32[1,16,256]{2,1,0:T(8,128)}, u32[]{:S(2)}) copy-start(f32[1,16,256]{2,1,0:T(8,128)} %param.11) | copy-start | bytes 49156
  7.2 559.4 %all-reduce.2.cloned.1.call-start = ((), (), s32[]{:S(2)}) async-start(), calls=%async_computation | async-start | bytes 688128 | tf_op jit(solution)/shard_map/psum | solution.py:156
  7.3 102.3 %collective-permute-start = (bf16[1,128,4096]{2,1,0:T(8,128)(2,1)}, bf16[1,128,4096]{2,1,0:T(8,128)(2,1)S(1)}, u32[]{:S(2)}, u32[]{:S(2)}) collective-permute-start(bf16[1,128,4096]{2,1,0:T(8,128)(2,1)} %param.7), channel_id=1, source_target_pairs={{0,1},{1,2},{2,3},{3,0},{4,5},{5,6},{6,7},{7,4},{8,9},{9,10},{10,1... | collective-permute-start | bytes 3145736 | tf_op jit(solution)/shard_map/ppermute | solution.py:17
  10.1 213.9 %collective-permute-start.3 = (bf16[1,128,4096]{1,2,0:T(8,128)(2,1)}, bf16[1,128,4096]{1,2,0:T(8,128)(2,1)S(1)}, u32[]{:S(2)}, u32[]{:S(2)}) collective-permute-start(bf16[1,128,4096]{1,2,0:T(8,128)(2,1)} %copy.91), channel_id=1, source_target_pairs={{0,3},{1,0},{2,1},{3,2},{4,7},{5,4},{6,5},{7,6},{8,11},{9,8},{10,9... | collective-permute-start | bytes 3145736 | tf_op jit(solution)/shard_map/ppermute | solution.py:17
  19.0 8.1 %copy-start.12 = (f32[16,256]{0,1:T(8,128)}, f32[16,256]{0,1:T(8,128)S(1)}, u32[]{:S(2)}) copy-start(f32[16,256]{0,1:T(8,128)S(1)} %copy.85) | copy-start | bytes 49156
  109.5 7.0 %copy-start.14 = (bf16[1,128,4096]{2,1,0:T(8,128)(2,1)}, bf16[1,128,4096]{2,1,0:T(8,128)(2,1)S(1)}, u32[]{:S(2)}) copy-start(bf16[1,128,4096]{2,1,0:T(8,128)(2,1)S(1)} %collective-permute-done) | copy-start | bytes 3145732
  109.6 7.0 %collective-permute-start.1 = (bf16[2,6,4096]{2,1,0:T(8,128)(2,1)S(1)}, bf16[2,6,4096]{2,1,0:T(8,128)(2,1)S(1)}, u32[]{:S(2)}, u32[]{:S(2)}) collective-permute-start(bf16[2,6,4096]{2,1,0:T(8,128)(2,1)S(1)} %pad_maximum_fusion.2), channel_id=1, source_target_pairs={{0,4},{4,8},{8,12},{12,16},{16,20},{20,24},{24,28},{1,5},{5,9},{9,... | collective-permute-start | bytes 294920 | tf_op jit(solution)/shard_map/ppermute | solution.py:12
  166.3 2.7 copy-start.2
  166.3 4.0 copy-start.34
  166.3 4.0 copy-start.44
  169.0 1.3 copy-start
  178.5 179.5 %collective-permute-start.2 = (f32[16,16,256]{2,1,0:T(8,128)}, f32[16,16,256]{2,1,0:T(8,128)}, u32[]{:S(2)}, u32[]{:S(2)}) collective-permute-start(f32[16,16,256]{2,1,0:T(8,128)} %copy.89), channel_id=1, source_target_pairs={{0,4},{4,8},{8,12},{12,16},{16,20},{20,24},{24,28},{1,5},{5,9},{9,... | collective-permute-start | bytes 786440 | tf_op jit(solution)/shard_map/ppermute | solution.py:12
  192.0 18.2 %copy-start.7 = (f32[4096,128]{1,0:T(8,128)}, f32[4096,128]{1,0:T(8,128)S(1)}, u32[]{:S(2)}) copy-start(f32[4096,128]{1,0:T(8,128)S(1)} %copy.97) | copy-start | bytes 6291460
  207.3 2.9 copy-start.15
  207.3 2.9 copy-start.17
  223.9 2.6 copy-start.1
  223.9 2.9 copy-start.30
  231.8 4.8 copy-start.23
  235.1 31.1 %collective-permute-start.5 = (f32[16,16,256]{2,1,0:T(8,128)}, f32[16,16,256]{2,1,0:T(8,128)}, u32[]{:S(2)}, u32[]{:S(2)}) collective-permute-start(f32[16,16,256]{2,1,0:T(8,128)} %copy.101), channel_id=1, source_target_pairs={{4,0},{8,4},{12,8},{16,12},{20,16},{24,20},{28,24},{5,1},{9,5},{13... | collective-permute-start | bytes 786440 | tf_op jit(solution)/shard_map/ppermute | solution.py:12
  266.1 3.5 copy-start.13
  269.6 22.5 %slice-start.4 = ((s8[6291456]{0:T(1024)(128)(4,1)}), s8[4194304]{0:T(1024)(128)(4,1)S(1)}, s32[]{:S(2)}) async-start(s8[6291456]{0:T(1024)(128)(4,1)} %bitcast.136), calls=%async_computation.5 | async-start | bytes 8388608
  274.3 17.8 %slice-start.5 = ((s8[6291456]{0:T(1024)(128)(4,1)}), s8[2097152]{0:T(1024)(128)(4,1)S(1)}, s32[]{:S(2)}) async-start(s8[6291456]{0:T(1024)(128)(4,1)} %bitcast.136), calls=%async_computation.6 | async-start | bytes 4194304
  274.4 22.0 %slice-start = ((s8[16777216]{0:T(1024)(128)(4,1)}), s8[4194304]{0:T(1024)(128)(4,1)S(1)}, s32[]{:S(2)}) async-start(s8[16777216]{0:T(1024)(128)(4,1)} %bitcast.124), calls=%async_computation.1 | async-start | bytes 8388608
  274.4 22.0 %slice-start.1 = ((s8[16777216]{0:T(1024)(128)(4,1)}), s8[4194304]{0:T(1024)(128)(4,1)S(1)}, s32[]{:S(2)}) async-start(s8[16777216]{0:T(1024)(128)(4,1)} %bitcast.124), calls=%async_computation.2 | async-start | bytes 8388608
  274.4 22.0 %slice-start.2 = ((s8[16777216]{0:T(1024)(128)(4,1)}), s8[4194304]{0:T(1024)(128)(4,1)S(1)}, s32[]{:S(2)}) async-start(s8[16777216]{0:T(1024)(128)(4,1)} %bitcast.124), calls=%async_computation.3 | async-start | bytes 8388608
  292.2 4.2 slice-start.3
  324.0 29.1 %copy-start.35 = (f32[128]{0:T(128)S(1)}, f32[128]{0:T(128)}, u32[]{:S(2)}) copy-start(f32[128]{0:T(128)} %iota_subtract_fusion.1) | copy-start | bytes 1540
  324.0 29.1 %copy-start.36 = (f32[128]{0:T(128)S(1)}, f32[128]{0:T(128)}, u32[]{:S(2)}) copy-start(f32[128]{0:T(128)} %compare_convert_fusion.7) | copy-start | bytes 1540
  358.1 3.4 copy-start.29
  358.1 3.4 copy-start.43
  368.7 8.5 %copy-start.33 = (f32[128]{0:T(128)S(1)}, f32[128]{0:T(128)}, u32[]{:S(2)}) copy-start(f32[128]{0:T(128)} %iota_add_fusion.1) | copy-start | bytes 1540
  372.0 37.5 %collective-permute-start.4 = (f32[16,16,256]{2,1,0:T(8,128)}, f32[16,16,256]{2,1,0:T(8,128)}, u32[]{:S(2)}, u32[]{:S(2)}) collective-permute-start(f32[16,16,256]{2,1,0:T(8,128)} %copy.99), channel_id=1, source_target_pairs={{0,4},{4,8},{8,12},{12,16},{16,20},{20,24},{24,28},{1,5},{5,9},{9,... | collective-permute-start | bytes 786440 | tf_op jit(solution)/shard_map/ppermute | solution.py:12
  407.2 5.7 copy-start.31
  412.8 6.7 %copy-start.8 = (f32[4096,128]{1,0:T(8,128)S(1)}, f32[4096,128]{1,0:T(8,128)}, u32[]{:S(2)}) copy-start(f32[4096,128]{1,0:T(8,128)} %copy-done.7) | copy-start | bytes 6291460
  412.8 6.7 %copy-start.9 = (f32[4096,128]{1,0:T(8,128)S(1)}, f32[4096,128]{1,0:T(8,128)}, u32[]{:S(2)}) copy-start(f32[4096,128]{1,0:T(8,128)} %copy.98) | copy-start | bytes 6291460
  412.8 6.7 %copy-start.10 = (f32[4096,128]{1,0:T(8,128)S(1)}, f32[4096,128]{1,0:T(8,128)}, u32[]{:S(2)}) copy-start(f32[4096,128]{1,0:T(8,128)} %copy.96) | copy-start | bytes 6291460
  419.3 2.3 copy-start.5
  419.3 3.0 copy-start.6
  419.3 3.0 copy-start.22
  419.5 19.7 %copy-start.3 = (f32[1,4096,128]{2,1,0:T(8,128)}, f32[1,4096,128]{2,1,0:T(8,128)S(1)}, u32[]{:S(2)}) copy-start(f32[1,4096,128]{2,1,0:T(8,128)S(1)} %fusion.36) | copy-start | bytes 6291460
  446.7 6.0 %copy-start.24 = (f32[16,256]{0,1:T(8,128)S(1)}, f32[16,256]{0,1:T(8,128)}, u32[]{:S(2)}) copy-start(f32[16,256]{0,1:T(8,128)} %fusion.34) | copy-start | bytes 49156
  446.7 49.5 %copy-start.26 = (f32[3,4096]{1,0:T(4,128)S(1)}, f32[3,4096]{1,0:T(4,128)}, u32[]{:S(2)}) copy-start(f32[3,4096]{1,0:T(4,128)} %get-tuple-element.29) | copy-start | bytes 147460
  446.7 51.3 %collective-permute-start.6 = (f32[3,6,4096]{2,1,0:T(8,128)S(1)}, f32[3,6,4096]{2,1,0:T(8,128)S(1)}, u32[]{:S(2)}, u32[]{:S(2)}) collective-permute-start(f32[3,6,4096]{2,1,0:T(8,128)S(1)} %copy.103), channel_id=1, source_target_pairs={{4,0},{8,4},{12,8},{16,12},{20,16},{24,20},{28,24},{5,1},{9,5},{13... | collective-permute-start | bytes 884744 | tf_op jit(solution)/shard_map/ppermute | solution.py:12
  498.0 4.0 copy-start.4
  502.1 9.3 %copy-start.16 = (f32[3,4096]{1,0:T(4,128)S(1)}, f32[3,4096]{1,0:T(4,128)}, u32[]{:S(2)}) copy-start(f32[3,4096]{1,0:T(4,128)} %get-tuple-element.96) | copy-start | bytes 147460
  502.1 9.3 %copy-start.18 = (f32[3,4096]{1,0:T(4,128)S(1)}, f32[3,4096]{1,0:T(4,128)}, u32[]{:S(2)}) copy-start(f32[3,4096]{1,0:T(4,128)} %get-tuple-element.97) | copy-start | bytes 147460
  502.1 9.3 %copy-start.19 = (f32[3,4096]{1,0:T(4,128)S(1)}, f32[3,4096]{1,0:T(4,128)}, u32[]{:S(2)}) copy-start(f32[3,4096]{1,0:T(4,128)} %get-tuple-element.98) | copy-start | bytes 147460
  502.1 9.3 %copy-start.20 = (f32[3,4096]{1,0:T(4,128)S(1)}, f32[3,4096]{1,0:T(4,128)}, u32[]{:S(2)}) copy-start(f32[3,4096]{1,0:T(4,128)} %get-tuple-element.99) | copy-start | bytes 147460
  502.1 9.3 %copy-start.21 = (f32[3,4096]{1,0:T(4,128)S(1)}, f32[3,4096]{1,0:T(4,128)}, u32[]{:S(2)}) copy-start(f32[3,4096]{1,0:T(4,128)} %get-tuple-element.100) | copy-start | bytes 147460
  511.4 30.8 %copy-start.11 = (f32[4096,128]{1,0:T(8,128)S(1)}, f32[4096,128]{1,0:T(8,128)}, u32[]{:S(2)}) copy-start(f32[4096,128]{1,0:T(8,128)} %get-tuple-element.40) | copy-start | bytes 6291460
  511.4 30.8 %copy-start.37 = (f32[128]{0:T(128)S(1)}, f32[128]{0:T(128)}, u32[]{:S(2)}) copy-start(f32[128]{0:T(128)} %get-tuple-element.67) | copy-start | bytes 1540
  511.4 30.8 %copy-start.38 = (f32[128]{0:T(128)S(1)}, f32[128]{0:T(128)}, u32[]{:S(2)}) copy-start(f32[128]{0:T(128)} %get-tuple-element.68) | copy-start | bytes 1540
  511.4 30.8 %copy-start.39 = (f32[128]{0:T(128)S(1)}, f32[128]{0:T(128)}, u32[]{:S(2)}) copy-start(f32[128]{0:T(128)} %get-tuple-element.69) | copy-start | bytes 1540
  511.4 30.8 %copy-start.40 = (f32[128]{0:T(128)S(1)}, f32[128]{0:T(128)}, u32[]{:S(2)}) copy-start(f32[128]{0:T(128)} %get-tuple-element.70) | copy-start | bytes 1540
  511.5 30.8 %copy-start.41 = (f32[128]{0:T(128)S(1)}, f32[128]{0:T(128)}, u32[]{:S(2)}) copy-start(f32[128]{0:T(128)} %get-tuple-element.71) | copy-start | bytes 1540
  511.5 30.8 %copy-start.42 = (f32[128]{0:T(128)S(1)}, f32[128]{0:T(128)}, u32[]{:S(2)}) copy-start(f32[128]{0:T(128)} %get-tuple-element.72) | copy-start | bytes 1540
Sparse Core Ops, SparseCore 0:
  498.1 68.4 all-reduce.1
where the time goes:
time: 580 us; the launch traced here: 575 us
  local copies, waits for them, and re-layouts  181 us (31%)
  matrix products  169 us (29%)
  other arithmetic  132 us (23%)
  blocking collectives  39.2 us (7%)
  starting transfers between devices  20.9 us (4%)
  waiting for transfers between devices  17.9 us (3%)
  between operations  15 us (3%)
    gather x2, local copies, waits for them, and re-layouts, on_device(): toeplitz = jnp.take(kernel, lag_index, axis=1)  80 us
    psum x1, blocking collectives, on_device(): summed = lax.psum((filter_term, tap_term), 'ctx')  39.2 us
    mul x12, local copies, waits for them, and re-layouts, featurize(): window * valid[None, :]  34.7 us
    reduce_sum x1, other arithmetic, on_device(): jnp.sum(taps_here[:, j][:, :, None] * ahead, axis=0) * valid_up[None, :]  30.8 us
    dot_general x1, matrix products, on_device(): inner_part = jnp.einsum('fts,mfs->mft', pair_grad, rising, precision=HIGH)  29.9 us
    dot_general x1, matrix products, on_device(): long_new = jnp.einsum('fts,fgs->fgt', toep_new, gated_new, precision=HIGH)  29.6 us
    dot_general x1, matrix products, on_device(): jnp.einsum('fgt,fgs->fts', grad_long, gated_old, precision=HIGH)  29.1 us
    dot_general x1, matrix products, on_device(): long_old = jnp.einsum('fts,fgs->fgt', toep_old, gated_old, precision=HIGH)  27.6 us
  transfers between devices with their start and end apart: 8, of which 2 were waited for; matrix products, arithmetic and copies ran while one was open for 74% of the time, Pallas kernels for 0%

commit v1 on v0

v1 whole, which is shorter than its diff:
```python
import functools
import jax
import jax.numpy as jnp
from jax import lax
from jax.experimental import pallas as pl
from jax.experimental.pallas import tpu as pltpu
from jax.sharding import PartitionSpec as P

F32 = jnp.float32
UNROLL = 4
LANES = 128
SUB = 8
BLOCK = LANES * SUB


def from_behind(value, axis, steps):
    count = lax.axis_size(axis)
    initial, last = (max(0, -steps), min(count, count - steps))
    return lax.ppermute(value, axis, [(source, source + steps) for source in range(initial, last)])


def passed_along(array, axis, by):
    count = lax.axis_size(axis)
    return lax.ppermute(array, axis, [(i, (i + by) % count) for i in range(count)])


def doc_meta(lengths, base, rows):
    starts = jnp.cumsum(lengths) - lengths
    places = base + jnp.arange(rows + 16, dtype=jnp.int32)
    far = jnp.int32(1 << 30)
    gaps = places[:, None] - starts[None, :]
    age = jnp.min(jnp.where(gaps >= 0, gaps, far), axis=1)
    keep = (age > 0).astype(jnp.int32)
    positions = jnp.arange(rows, dtype=jnp.int32)
    fresh = age[:rows] == 0
    first = jnp.min(jnp.where(fresh, positions, rows))
    last = jnp.max(jnp.where(fresh, positions, -1))
    through = first == rows
    u = UNROLL
    front_hi = (first + u - 1) // u
    main_lo = jnp.where(through, 0, first // u)
    main_hi = jnp.where(through, rows // u, (last + u - 1) // u)
    tail_lo = jnp.maximum(last, 0) // u
    bounds = jnp.stack([front_hi, main_lo, main_hi, tail_lo, last, age[0]]).astype(jnp.int32)
    return jnp.concatenate([bounds, jnp.zeros((2,), jnp.int32), keep]), through.astype(F32)


HEAD = 8


def at(ref, t):
    return ref[pl.ds(pl.multiple_of(t * SUB, SUB), SUB), :]


def put(ref, t, value):
    ref[pl.ds(pl.multiple_of(t * SUB, SUB), SUB), :] = value


def scatter_rows(src, dst, rows, offset):
    def body(g, _):
        for c in range(SUB):
            tile = src[pl.ds(pl.multiple_of(g * 16, 16), 16), c * LANES : (c + 1) * LANES].astype(F32)
            for h in range(2):
                dst[pl.ds((offset + g * 16 + h * 8) * SUB + c, 8, stride=SUB), :] = tile[h * 8 : h * 8 + 8]
        return 0

    lax.fori_loop(0, rows // 16, body, 0)


def gather_rows(src, dst, rows):
    def body(g, _):
        for c in range(SUB):
            halves = [src[pl.ds((g * 16 + h * 8) * SUB + c, 8, stride=SUB), :] for h in range(2)]
            dst[pl.ds(pl.multiple_of(g * 16, 16), 16), c * LANES : (c + 1) * LANES] = jnp.concatenate(
                halves, axis=0
            ).astype(dst.dtype)
        return 0

    lax.fori_loop(0, rows // 16, body, 0)


def total_of(parts):
    while len(parts) > 1:
        parts = [a + b for a, b in zip(parts[::2], parts[1::2])] + ([parts[-1]] if len(parts) % 2 else [])
    return parts[0]


def decayed(dtab, flag, states, value):
    modes = len(states)
    return [
        states[m] * dtab[pl.ds(pl.multiple_of(flag * (modes * SUB) + m * SUB, SUB), SUB), :] + value
        for m in range(modes)
    ]


def load_states(ref, modes):
    return tuple(at(ref, m) for m in range(modes))


def scan_forward(meta, source, dtab, resid, lo, hi, init, emit):
    modes = len(init)

    def body(g, states):
        states = list(states)
        for u in range(UNROLL):
            t = g * UNROLL + u
            states = decayed(dtab, meta[HEAD + t], states, at(source, t))
            emit(t, total_of([at(resid, m) * states[m] for m in range(modes)]))
        return tuple(states)

    return lax.fori_loop(lo, hi, body, init)


def scan_backward(meta, cotan, source, dtab, resid, lo, hi, init, totals, weight, emit):
    modes = len(init)

    def body(i, carry):
        states, sums = list(carry[0]), list(carry[1])
        g = hi - 1 - i
        for u in reversed(range(UNROLL)):
            t = g * UNROLL + u
            states = decayed(dtab, meta[HEAD + t + 1], states, at(cotan, t))
            emit(t, total_of([at(resid, m) * states[m] for m in range(modes)]))
            value = at(source, t) * weight(t)
            sums = [sums[m] + value * states[m] for m in range(modes)]
        return tuple(states), tuple(sums)

    return lax.fori_loop(0, hi - lo, body, (init, totals))


def forward_kernel(rows, modes, taps_count, meta, x, rim, taps, dtab, resid, *outs, full):
    if full:
        xs, qs, ks, vs, gs, longs, end = outs
    else:
        qs, gs, longs, end, xs = outs
    for c in range(SUB):
        xs[pl.ds(c, 8, stride=SUB), :] = rim[:, c * LANES : (c + 1) * LANES].astype(F32)
    scatter_rows(x, xs, rows, 8)
    age = meta[5]
    window = tuple(
        at(xs, 8 - j) * jnp.where(age >= j, 1.0, 0.0).astype(F32) for j in range(1, taps_count)
    )

    def feats(g, window):
        window = list(window)
        for u in range(2):
            t = g * 2 + u
            keep = meta[HEAD + t].astype(F32)
            now = at(xs, t + 8)
            seen = [now] + [w * keep for w in window]
            q, k, v = [
                total_of([at(taps, i * taps_count + j) * seen[j] for j in range(taps_count)])
                for i in range(3)
            ]
            put(qs, t, q)
            put(gs, t, k * v)
            if full:
                put(ks, t, k)
                put(vs, t, v)
            window = seen[:-1]
        return tuple(window)

    lax.fori_loop(0, rows // 2, feats, window)
    init = tuple(jnp.zeros((SUB, LANES), F32) for _ in range(modes))
    states = scan_forward(
        meta, gs, dtab, resid, meta[1], rows // UNROLL, init, lambda t, y: put(longs, t, y)
    )
    for m in range(modes):
        put(end, m, states[m])


def mixed_kernel(rows, modes, meta, qs, gs, longs, state, dtab, resid, out, scratch):
    def product(g, _):
        for u in range(8):
            t = g * 8 + u
            put(scratch, t, at(qs, t) * at(longs, t))
        return 0

    lax.fori_loop(0, rows // 8, product, 0)
    scan_forward(
        meta, gs, dtab, resid, 0, meta[0], load_states(state, modes),
        lambda t, y: put(scratch, t, y * at(qs, t)),
    )
    gather_rows(scratch, out, rows)


def backward_kernel(
    rows, modes, meta, up, qs, ks, vs, gs, longs, state, dtab, resid,
    dq, dl, dg, begin, sums, rim, ups,
):
    scatter_rows(up, ups, rows, 0)

    def product(g, _):
        for u in range(8):
            t = g * 8 + u
            value = at(ups, t)
            put(dq, t, value * at(longs, t))
            put(dl, t, value * at(qs, t))
            put(dg, t, jnp.zeros((SUB, LANES), F32))
        return 0

    lax.fori_loop(0, rows // 8, product, 0)
    scan_forward(
        meta, gs, dtab, resid, 0, meta[0], load_states(state, modes),
        lambda t, y: put(dq, t, y * at(ups, t)),
    )
    zeros = tuple(jnp.zeros((SUB, LANES), F32) for _ in range(modes))
    last = meta[4]
    states, totals = scan_backward(
        meta, dl, gs, dtab, resid, 0, meta[2], zeros, zeros,
        lambda t: jnp.where(t < last, 1.0, 0.0).astype(F32),
        lambda t, y: put(dg, t, y),
    )
    for m in range(modes):
        put(begin, m, states[m])
        put(sums, m, totals[m])
    for t in range(8):
        value = at(dg, t)
        put(rim, t, at(dq, t))
        put(rim, 8 + t, value * at(vs, t))
        put(rim, 16 + t, value * at(ks, t))


def finish_kernel(
    rows, modes, taps_count, meta, xs, ks, vs, gs, dq, dl, dg, rim, state, sums, taps, dtab, resid,
    out, tap_out, sums_out, dks, dvs, backs,
):
    def copy(g, _):
        for u in range(8):
            put(dks, g * 8 + u, at(dg, g * 8 + u))
        return 0

    lax.fori_loop(0, rows // 8, copy, 0)
    last = meta[4]
    _, totals = scan_backward(
        meta, dl, gs, dtab, resid, meta[3], rows // UNROLL, load_states(state, modes),
        load_states(sums, modes),
        lambda t: jnp.where(t >= last, 1.0, 0.0).astype(F32),
        lambda t, y: put(dks, t, y),
    )
    for m in range(modes):
        put(sums_out, m, totals[m])

    def spread(pending, grads, keep):
        parts = [
            total_of([at(taps, i * taps_count + j) * grads[i] for i in range(3)])
            for j in range(taps_count)
        ]
        done = pending[0] + parts[0]
        later = list(pending[1:]) + [None]
        return done, tuple(
            ((parts[k + 1] + later[k]) if later[k] is not None else parts[k + 1]) * keep
            for k in range(taps_count - 1)
        )

    pending = tuple(jnp.zeros((SUB, LANES), F32) for _ in range(taps_count - 1))
    for r in reversed(range(taps_count - 1)):
        grads = [at(rim, i * 8 + r) for i in range(3)]
        _, pending = spread(pending, grads, meta[HEAD + rows + r].astype(F32))

    def descend(i, pending):
        g = rows // 2 - 1 - i
        for u in reversed(range(2)):
            t = g * 2 + u
            gated = at(dks, t)
            dk = gated * at(vs, t)
            dv = gated * at(ks, t)
            put(dks, t, dk)
            put(dvs, t, dv)
            done, pending = spread(pending, [at(dq, t), dk, dv], meta[HEAD + t].astype(F32))
            put(backs, t, done)
        return pending

    lax.fori_loop(0, rows // 2, descend, pending)
    gather_rows(backs, out, rows)
    age = meta[5]
    window = tuple(
        at(xs, 8 - j) * jnp.where(age >= j, 1.0, 0.0).astype(F32) for j in range(1, taps_count)
    )
    zeros = tuple(jnp.zeros((SUB, LANES), F32) for _ in range(3 * taps_count))

    def ascend(g, carry):
        window, acc = list(carry[0]), list(carry[1])
        for u in range(2):
            t = g * 2 + u
            keep = meta[HEAD + t].astype(F32)
            seen = [at(xs, t + 8)] + [w * keep for w in window]
            grads = [at(dq, t), at(dks, t), at(dvs, t)]
            acc = [
                acc[i * taps_count + j] + grads[i] * seen[j]
                for i in range(3)
                for j in range(taps_count)
            ]
            window = seen[:-1]
        return tuple(window), tuple(acc)

    _, acc = lax.fori_loop(0, rows // 2, ascend, (window, zeros))
    for n in range(3 * taps_count):
        put(tap_out, n, acc[n])


def on_device(section_out, stash, grad_out, taps, residues, decays, doc_lengths):
    stashed = stash[0]
    rows, width = stashed.shape
    modes, filters = residues.shape[1:]
    branches, taps_count = taps.shape[1:3]
    group = width // filters
    blocks = width // BLOCK
    ctx_size = lax.axis_size("ctx")
    pipe_size = lax.axis_size("pipe")
    base = lax.axis_index("ctx") * rows
    span = rows * ctx_size // 16 // rows + 1
    depth = (span - 1).bit_length()

    upstream = passed_along(grad_out, "pipe", -1)[0]
    incoming = passed_along(section_out, "pipe", 1)[0]
    rim_old = from_behind(stashed[rows - 8 :], "ctx", 1)
    rim_new = from_behind(passed_along(section_out[0, rows - 8 :], "pipe", 1), "ctx", 1)

    meta_new, through_new = doc_meta(doc_lengths[0], base, rows)
    meta_old, through_old = doc_meta(doc_lengths[1], base, rows)

    def expand(small):
        wide = jnp.broadcast_to(small[:, :, None], (modes, filters, group)).reshape(modes, blocks, SUB, LANES)
        return jnp.swapaxes(wide, 0, 1).reshape(blocks, modes * SUB, LANES)

    rates = expand(decays[0])
    resid = expand(residues[0])
    decay = jnp.exp(-rates)
    dtab = jnp.concatenate([jnp.zeros_like(decay), decay], axis=1)
    tapped = jnp.swapaxes(taps[0].reshape(branches * taps_count, blocks, SUB, LANES), 0, 1)
    tapped = tapped.reshape(blocks, branches * taps_count * SUB, LANES)

    smem = pl.BlockSpec(memory_space=pltpu.SMEM)
    tokens = pl.BlockSpec((rows, BLOCK), lambda b: (0, b))
    edge = pl.BlockSpec((8, BLOCK), lambda b: (0, b))

    def major(count):
        return pl.BlockSpec((None, count * SUB, LANES), lambda b: (b, 0, 0))

    def shaped(count):
        return jax.ShapeDtypeStruct((blocks, count * SUB, LANES), F32)

    def scratch(count):
        return pltpu.VMEM((count * SUB, LANES), F32)

    def cost(ops, count):
        return pl.CostEstimate(flops=ops * rows * width, bytes_accessed=4 * count * rows * width, transcendentals=0)

    wide = jax.ShapeDtypeStruct((rows, width), jnp.bfloat16)
    tail = [major(branches * taps_count), major(2 * modes), major(modes)]

    def link(earlier, later):
        return (earlier[0] * later[0], later[0] * earlier[1] + later[1])

    def nearby(through, summary, sign):
        if depth == 0:
            return from_behind(summary, "ctx", sign)
        current = (through * jnp.exp(-rates * rows), summary)
        for j in range(depth + 1):
            reach = 1 if j == 0 else 2 ** (j - 1)
            moved = from_behind(current, "ctx", sign * reach)
            current = moved if j == 0 else link(moved, current)
        return current[1]

    xs, qs, ks, vs, gs, longs, end_old = pl.pallas_call(
        functools.partial(forward_kernel, rows, modes, taps_count, full=True),
        grid=(blocks,),
        in_specs=[smem, tokens, edge] + tail,
        out_specs=[major(rows + 8)] + [major(rows)] * 5 + [major(modes)],
        out_shape=[shaped(rows + 8)] + [shaped(rows)] * 5 + [shaped(modes)],
        cost_estimate=cost(110, 7),
        name="forward_old",
    )(meta_old, stashed, rim_old, tapped, dtab, resid)
    state_old = nearby(through_old, end_old, 1)

    qn, gn, longn, end_new = pl.pallas_call(
        functools.partial(forward_kernel, rows, modes, taps_count, full=False),
        grid=(blocks,),
        in_specs=[smem, tokens, edge] + tail,
        out_specs=[major(rows)] * 3 + [major(modes)],
        out_shape=[shaped(rows)] * 3 + [shaped(modes)],
        scratch_shapes=[scratch(rows + 8)],
        cost_estimate=cost(110, 4),
        name="forward_new",
    )(meta_new, incoming, rim_new, tapped, dtab, resid)
    state_new = nearby(through_new, end_new, 1)

    dq, dl, dg, begin, sums, rim = pl.pallas_call(
        functools.partial(backward_kernel, rows, modes),
        grid=(blocks,),
        in_specs=[smem, tokens] + [major(rows)] * 5 + [major(modes)] + tail[1:],
        out_specs=[major(rows)] * 3 + [major(modes)] * 2 + [major(24)],
        out_shape=[shaped(rows)] * 3 + [shaped(modes)] * 2 + [shaped(24)],
        scratch_shapes=[scratch(rows)],
        cost_estimate=cost(120, 8),
        name="backward_main",
    )(meta_old, upstream, qs, ks, vs, gs, longs, state_old, dtab, resid)
    later = nearby(through_old, begin, -1)
    if depth > 0:
        reach = (rows - jnp.arange(8, dtype=F32))[None, :, None, None, None]
        spread = (blocks, modes, SUB, LANES)
        extra = jnp.sum(
            (resid * later).reshape(spread)[:, None]
            * jnp.exp(-rates.reshape(spread)[:, None] * jnp.swapaxes(reach, 2, 2)),
            axis=2,
        ).reshape(blocks, 8 * SUB, LANES) * through_old
        head = 8 * SUB
        rim = rim + jnp.concatenate(
            [jnp.zeros_like(extra), extra * vs[:, :head], extra * ks[:, :head]], axis=1
        )
    rim_in = from_behind(rim, "ctx", -1)

    mixed = pl.pallas_call(
        functools.partial(mixed_kernel, rows, modes),
        grid=(blocks,),
        in_specs=[smem] + [major(rows)] * 3 + [major(modes)] + tail[1:],
        out_specs=tokens,
        out_shape=wide,
        scratch_shapes=[scratch(rows)],
        cost_estimate=cost(30, 4),
        name="mixed",
    )(meta_new, qn, gn, longn, state_new, dtab, resid)

    back, tap_term, totals = pl.pallas_call(
        functools.partial(finish_kernel, rows, modes, taps_count),
        grid=(blocks,),
        in_specs=[smem, major(rows + 8)] + [major(rows)] * 6 + [major(24)] + [major(modes)] * 2 + tail,
        out_specs=[tokens, major(branches * taps_count), major(modes)],
        out_shape=[wide, shaped(branches * taps_count), shaped(modes)],
        scratch_shapes=[scratch(rows)] * 3,
        cost_estimate=cost(150, 8),
        name="finish",
    )(meta_old, xs, ks, vs, gs, dq, dl, dg, rim_in, later, sums, tapped, dtab, resid)

    filter_term = jnp.sum(
        jnp.swapaxes(totals.reshape(blocks, modes, SUB, LANES), 0, 1).reshape(modes, filters, group), axis=2
    )
    tap_term = jnp.swapaxes(tap_term.reshape(blocks, branches * taps_count, SUB, LANES), 0, 1).reshape(
        branches, taps_count, width
    )
    summed = lax.psum((filter_term, tap_term), "ctx")
    return (mixed[None], back[None], summed[0][None], summed[1][None])


def solution(mesh):
    in_specs = (
        P("pipe", "ctx", None),
        P("pipe", "ctx", None),
        P("pipe", "ctx", None),
        P("pipe", None, None, None),
        P("pipe", None, None),
        P("pipe", None, None),
        P(),
    )
    out_specs = (
        P("pipe", "ctx", None),
        P("pipe", "ctx", None),
        P("pipe", None, None),
        P("pipe", None, None, None),
    )
    return jax.shard_map(
        on_device, mesh=mesh, in_specs=in_specs, out_specs=out_specs, check_vma=False
    )
```

time: 580 us -> 213 us (0.37)
  matrix products: 169 us -> 0 us
  local copies, waits for them, and re-layouts: 181 us -> 22.6 us
  other arithmetic: 132 us -> 4.47 us
  Pallas kernels: 0 us -> 61.9 us
  waiting for transfers between devices: 17.9 us -> 42.3 us
  between operations: 15 us -> 24.8 us
    dot_general x12 -> x0, matrix products: 169 us -> none  [the longest x1 29.9 us: on_device(): inner_part = jnp.einsum('fts,mfs->mft', pair_grad, rising, precision=HIGH)]
    gather x2 -> x0, local copies, waits for them, and re-layouts: 80 us -> none  [on_device(): toeplitz = jnp.take(kernel, lag_index, axis=1)]
    pallas_call x0 -> x5, Pallas kernels: none -> 61.9 us  [the longest x2 28.7 us: on_device(): pl.pallas_call(functools.partial(forward_kernel, rows, modes, taps_count,...]
    reduce_sum x4 -> x1, other arithmetic: 49.4 us -> 0.61 us  [on_device(): jnp.sum(jnp.swapaxes(totals.reshape(blocks, modes, SUB, LANES), 0, 1).res...]
    mul x13 -> x0, local copies, waits for them, and re-layouts: 34.8 us -> none  [the longest x12 34.7 us: featurize(): window * valid[None, :]]
    add x4 -> x1, other arithmetic: 28 us -> 0.01 us  [doc_meta(): places = base + jnp.arange(rows + 16, dtype=jnp.int32)]
    slice x2 -> x0, other arithmetic: 17.9 us -> none  [featurize(): window = ext_cols[:, 6 - j:6 - j + rows]]
    unnamed x112 -> x27, local copies, waits for them, and re-layouts: 21.4 us -> 5.56 us
  transfers between devices with their start and end apart: 8 -> 10, of which waited for: 2 -> 3; matrix products, arithmetic and copies ran while one was open for 74% -> 10% of each run, Pallas kernels for 0% -> 29%
where the time goes in v1:
time: 213 us; the launch traced here: 214 us
  Pallas kernels  61.9 us (29%)
  waiting for transfers between devices  42.3 us (20%)
  blocking collectives  36.5 us (17%)
  between operations  24.8 us (12%)
  local copies, waits for them, and re-layouts  22.6 us (11%)
  starting transfers between devices  21.4 us (10%)
  other arithmetic  4.47 us (2%)
    psum x1, blocking collectives, on_device(): summed = lax.psum((filter_term, tap_term), 'ctx')  36.5 us
    psum x1, waiting for transfers between devices, on_device(): summed = lax.psum((filter_term, tap_term), 'ctx')  31.2 us
    pallas_call x2, Pallas kernels, on_device(): pl.pallas_call(functools.partial(forward_kernel, rows, modes, taps_count,...  28.7 us
    ppermute x6, starting transfers between devices, from_behind(): lax.ppermute(value, axis, [(source, source + steps) for source in range(i...  19.9 us
    pallas_call x1, Pallas kernels, on_device(): pl.pallas_call(functools.partial(finish_kernel, rows, modes, taps_count),...  15.9 us
    pallas_call x1, Pallas kernels, on_device(): pl.pallas_call(functools.partial(backward_kernel, rows, modes), grid=(blo...  12.4 us
    ppermute x6, waiting for transfers between devices, from_behind(): lax.ppermute(value, axis, [(source, source + steps) for source in range(i...  11.1 us
    unnamed x27, local copies, waits for them, and re-layouts  5.56 us
  transfers between devices with their start and end apart: 10, of which 3 were waited for; matrix products, arithmetic and copies ran while one was open for 10% of the time, Pallas kernels for 29%

profile of v1, /device:TPU:0, one launch (start us, length us, event | category | flops | bytes accessed | tf_op | source)
XLA Modules:
  0.0 213.9 jit_solution(5130913550656110804)
XLA Ops:
  7.2 0.0 all-reduce.3.cloned.1.call-start
  7.2 0.8 slice_bitcast_fusion
  8.1 4.9 %collective-permute-start.4 = (bf16[8,4096]{1,0:T(8,128)(2,1)S(1)}, bf16[8,4096]{1,0:T(8,128)(2,1)S(1)}, u32[]{:S(2)}, u32[]{:S(2)}) collective-permute-start(bf16[8,4096]{1,0:T(8,128)(2,1)S(1)} %slice_bitcast_fusion), channel_id=1, source_target_pairs={{0,4},{4,8},{8,12},{12,16},{16,20},{20,24},{24,28},{1,5},{5,9},{9,... | collective-permute-start | bytes 196616 | tf_op jit(solution)/shard_map/ppermute | solution.py:19
  12.9 0.7 collective-permute-start.5
  13.7 0.0 collective-permute-start
  13.7 0.8 fusion.6
  14.4 0.2 reduce-window_1_clone.1
  14.6 0.2 reduce-window_clone.1
  14.8 0.8 subtract_bitcast_fusion.1
  15.6 0.7 fusion.1
  16.2 0.6 compare_convert_fusion
  16.8 0.7 exponential_bitcast_fusion
  17.5 0.6 broadcast_in_dim.46
  18.1 0.6 exp.14
  18.7 0.7 copy_bitcast_fusion.3
  19.4 0.6 broadcast_in_dim.48
  20.0 0.0 copy-start.9
  20.0 0.0 copy-start.11
  20.0 0.0 copy-start.12
  20.1 0.6 reshape.56
  20.6 0.7 copy_bitcast_fusion.2.resid
  21.3 0.8 fusion.3
  27.4 0.6 slice.33
  27.9 1.7 copy.27
  29.7 1.8 concatenate.10.dtab
  31.5 2.0 concatenate.11.meta
  33.5 0.0 collective-permute-done.4.rim
  33.5 0.6 copy-done.6
  34.1 14.5 %forward_old.1 = (f32[4,1088,128]{2,1,0:T(8,128)}, f32[4,1024,128]{2,1,0:T(8,128)}, f32[4,1024,128]{2,1,0:T(8,128)}, f32[4,1024,128]{2,1,0:T(8,128)}, f32[4,1024...) custom-call(s32[152]{0:T(256)} %concatenate.11.meta, bf16[128,4096]{1,0:T(8,128)(2,1)} %bitcast.58, ...), custom_call_target="tpu_custom_call" | custom-call | flops 57671680 | bytes 14680064 | tf_op jit(solution)/shard_map/forward_old/pallas_call | solution.py:366
  48.6 1.5 collective-permute-start.6
  50.2 0.8 slice_bitcast_fusion.1
  51.0 0.8 collective-permute-start.1
  51.8 5.3 %collective-permute-done.6.state = f32[4,128,128]{2,1,0:T(8,128)S(1)} collective-permute-done((f32[4,128,128]{2,1,0:T(8,128)}, f32[4,128,128]{2,1,0:T(8,128)S(1)}, u32[]{:S(2)}, u32[]{:S(2)}) %collective-permute-start.6) | collective-permute-done | bytes 262176 | tf_op jit(solution)/shard_map/ppermute | solution.py:19
  57.0 0.0 collective-permute-done.5
  57.1 0.7 copy-done.4
  57.8 0.3 copy-done
  58.1 12.4 %backward_main.1 = (f32[4,1024,128]{2,1,0:T(8,128)}, f32[4,1024,128]{2,1,0:T(8,128)}, f32[4,1024,128]{2,1,0:T(8,128)}, f32[4,128,128]{2,1,0:T(8,128)}, f32[4,128,128]{2,1,0:T(8,128)}, /*index=5*/f32[4,192,128]{2,1,0:T(8,128)}) custom-call(s32[152]{0:T(256)} %concatenate.11.meta, bf16[128,4096]{1,0:T(8,128)(2,1)} %bitcast.59, ...), custom_call_target="tpu_custom_call" | custom-call | flops 62914560 | bytes 16777216 | tf_op jit(solution)/shard_map/backward_main/pallas_call | solution.py:389
  70.5 1.3 collective-permute-start.7
  71.8 0.0 collective-permute-done.1
  71.8 6.7 %collective-permute-start.2 = (bf16[8,4096]{1,0:T(8,128)(2,1)S(1)}, bf16[8,4096]{1,0:T(8,128)(2,1)S(1)}, u32[]{:S(2)}, u32[]{:S(2)}) collective-permute-start(bf16[8,4096]{1,0:T(8,128)(2,1)S(1)} %collective-permute-done.1), channel_id=1, source_target_pairs={{0,4},{4,8},{8,12},{12,16},{16,20},{20,24},{24,28},{1,5},{5,9},{9,... | collective-permute-start | bytes 196616 | tf_op jit(solution)/shard_map/ppermute | solution.py:19
  78.5 1.3 collective-permute-start.8
  85.0 0.5 slice.29
  85.6 1.9 concatenate.9.meta
  87.5 5.8 %collective-permute-done.2.rim = bf16[8,4096]{1,0:T(8,128)(2,1)S(1)} collective-permute-done((bf16[8,4096]{1,0:T(8,128)(2,1)S(1)}, bf16[8,4096]{1,0:T(8,128)(2,1)S(1)}, u32[]{:S(2)}, u32[]{:S(2)}) %collective-permute-start.2) | collective-permute-done | bytes 65568 | tf_op jit(solution)/shard_map/ppermute | solution.py:19
  93.3 0.0 collective-permute-done
  93.3 0.6 copy-done.7
  93.9 14.1 %forward_new.1 = (f32[4,1024,128]{2,1,0:T(8,128)}, f32[4,1024,128]{2,1,0:T(8,128)}, f32[4,1024,128]{2,1,0:T(8,128)}, f32[4,128,128]{2,1,0:T(8,128)}) custom-call(s32[152]{0:T(256)} %concatenate.9.meta, bf16[128,4096]{1,0:T(8,128)(2,1)} %bitcast.6.x, bf16[8,4096]{1,0:T(8,128)(2,1)} %copy-done.7, f32[4,168,128]{2,1,0:T(8,128)} %bitcast.55, ...), custom_call_target="tpu_custom_call" | custom-call | flops 57671680 | bytes 8388608 | tf_op jit(solution)/shard_map/forward_new/pallas_call | solution.py:377
  108.1 4.2 %collective-permute-start.3 = (f32[4,128,128]{2,1,0:T(8,128)}, f32[4,128,128]{2,1,0:T(8,128)S(1)}, u32[]{:S(2)}, u32[]{:S(2)}) collective-permute-start(f32[4,128,128]{2,1,0:T(8,128)} %get-tuple-element.27), channel_id=1, source_target_pairs={{0,4},{4,8},{8,12},{12,16},{16,20},{20,24},{24,28},{1,5},{5,9},{9,... | collective-permute-start | bytes 786440 | tf_op jit(solution)/shard_map/ppermute | solution.py:19
  112.3 0.0 collective-permute-done.8.state
  112.3 0.0 collective-permute-done.7.rim
  112.3 0.0 copy-start.1
  112.3 0.7 copy-done.2
  113.0 0.1 copy-done.1
  113.1 15.9 %finish.1 = (bf16[128,4096]{1,0:T(8,128)(2,1)}, f32[4,168,128]{2,1,0:T(8,128)}, f32[4,128,128]{2,1,0:T(8,128)}) custom-call(s32[152]{0:T(256)} %concatenate.11.meta, f32[4,1088,128]{2,1,0:T(8,128)} %get-tuple-element.28.xs, f32[4,1024,128]{2,1,0:T(8,128)} %get-tuple-element.29.ks, f32[4,1024,128]{2,1,0:T(8,128)} %get-tuple-element.30.vs, ...), custom_call_target="tpu_custom_call" | custom-call | flops 78643200 | bytes 16777216 | tf_op jit(solution)/shard_map/finish/pallas_call | solution.py:425
  129.1 1.7 copy.22
  130.8 0.0 all-reduce.3.cloned.1.call-update
  130.8 0.0 collective-permute-done.3.state
  130.8 0.7 copy-done.3
  131.5 4.9 %mixed.1 = bf16[128,4096]{1,0:T(8,128)(2,1)} custom-call(s32[152]{0:T(256)} %concatenate.9.meta, f32[4,1024,128]{2,1,0:T(8,128)} %get-tuple-element.24.qs, f32[4,1024,128]{2,1,0:T(8,128)} %get-tuple-element.25.gs, f32[4,1024,128]{2,1,0:T(8,128)} %get-tuple-element.26.longs, f32[4,128,128]{2,1,0:T(8,128)} %copy-done.3, f32[4,256,128]{2,1,0:T(8,128)} %concatenate.10.dtab, ...), custom_call_target="tpu_custom_call" | custom-call | flops 15728640 | bytes 8388608 | tf_op jit(solution)/shard_map/mixed/pallas_call | solution.py:414
  136.5 0.6 reshape.59
  137.1 0.6 reduce_sum.9
  137.7 36.5 %psum.14 = f32[1,16,256]{2,1,0:T(8,128)} all-reduce(f32[1,16,256]{2,1,0:T(8,128)S(1)} %bitcast.63), channel_id=1, replica_groups=mesh['ctx'=8,'pipe'=4] {'ctx'}, use_global_device_ids=true, to_apply=%region_9.10 | all-reduce | flops 4096 | bytes 32768 | tf_op jit(solution)/shard_map/psum | solution.py:442
  174.2 31.2 %all-reduce.3.cloned.1.call-done = f32[1,3,7,4096]{3,0,2,1:T(1,128)} async-done(((f32[1,3,7,4096]{3,0,2,1:T(1,128)}), f32[1,3,7,4096]{3,0,2,1:T(1,128)}) %all-reduce.3.cloned.1.call-update) | async-done | bytes 344080 | tf_op jit(solution)/shard_map/psum | solution.py:442
  205.4 1.7 copy.29
  (19 shorter events, 0.1 us)
Async XLA Ops:
  7.2 198.2 %all-reduce.3.cloned.1.call-start = ((), (), s32[]{:S(2)}) async-start(), calls=%async_computation | async-start | bytes 688128 | tf_op jit(solution)/shard_map/psum | solution.py:442
  8.1 25.4 %collective-permute-start.4 = (bf16[8,4096]{1,0:T(8,128)(2,1)S(1)}, bf16[8,4096]{1,0:T(8,128)(2,1)S(1)}, u32[]{:S(2)}, u32[]{:S(2)}) collective-permute-start(bf16[8,4096]{1,0:T(8,128)(2,1)S(1)} %slice_bitcast_fusion), channel_id=1, source_target_pairs={{0,4},{4,8},{8,12},{12,16},{16,20},{20,24},{24,28},{1,5},{5,9},{9,... | collective-permute-start | bytes 196616 | tf_op jit(solution)/shard_map/ppermute | solution.py:19
  12.9 44.1 %collective-permute-start.5 = (bf16[1,128,4096]{2,1,0:T(8,128)(2,1)}, bf16[1,128,4096]{2,1,0:T(8,128)(2,1)S(1)}, u32[]{:S(2)}, u32[]{:S(2)}) collective-permute-start(bf16[1,128,4096]{2,1,0:T(8,128)(2,1)} %param.9), channel_id=1, source_target_pairs={{0,3},{1,0},{2,1},{3,2},{4,7},{5,4},{6,5},{7,6},{8,11},{9,8},{10,9... | collective-permute-start | bytes 3145736 | tf_op jit(solution)/shard_map/ppermute | solution.py:24
  13.7 79.6 %collective-permute-start = (bf16[1,128,4096]{2,1,0:T(8,128)(2,1)}, bf16[1,128,4096]{2,1,0:T(8,128)(2,1)}, u32[]{:S(2)}, u32[]{:S(2)}) collective-permute-start(bf16[1,128,4096]{2,1,0:T(8,128)(2,1)} %param.7), channel_id=1, source_target_pairs={{0,1},{1,2},{2,3},{3,0},{4,5},{5,6},{6,7},{7,4},{8,9},{9,10},{10,1... | collective-permute-start | bytes 3145736 | tf_op jit(solution)/shard_map/ppermute | solution.py:24
  16.2 0.6 copy-start.10
  17.5 1.9 copy-start.8
  20.0 1.3 copy-start.9
  20.0 1.3 copy-start.11
  20.0 11.4 %copy-start.12 = (s32[144]{0:T(256)S(1)}, s32[144]{0:T(256)}, u32[]{:S(2)}) copy-start(s32[144]{0:T(256)} %compare_convert_fusion) | copy-start | bytes 1732
  33.5 0.6 copy-start.6
  48.6 8.4 %collective-permute-start.6 = (f32[4,128,128]{2,1,0:T(8,128)}, f32[4,128,128]{2,1,0:T(8,128)S(1)}, u32[]{:S(2)}, u32[]{:S(2)}) collective-permute-start(f32[4,128,128]{2,1,0:T(8,128)} %get-tuple-element.34), channel_id=1, source_target_pairs={{0,4},{4,8},{8,12},{12,16},{16,20},{20,24},{24,28},{1,5},{5,9},{9,... | collective-permute-start | bytes 786440 | tf_op jit(solution)/shard_map/ppermute | solution.py:19
  51.0 20.8 %collective-permute-start.1 = (bf16[8,4096]{1,0:T(8,128)(2,1)S(1)}, bf16[8,4096]{1,0:T(8,128)(2,1)S(1)}, u32[]{:S(2)}, u32[]{:S(2)}) collective-permute-start(bf16[8,4096]{1,0:T(8,128)(2,1)S(1)} %slice_bitcast_fusion.1), channel_id=1, source_target_pairs={{0,1},{1,2},{2,3},{3,0},{4,5},{5,6},{6,7},{7,4},{8,9},{9,10},{10,1... | collective-permute-start | bytes 196616 | tf_op jit(solution)/shard_map/ppermute | solution.py:24
  57.0 0.7 copy-start.4
  57.1 1.1 copy-start
  70.5 41.8 %collective-permute-start.7 = (f32[4,192,128]{2,1,0:T(8,128)}, f32[4,192,128]{2,1,0:T(8,128)S(1)}, u32[]{:S(2)}, u32[]{:S(2)}) collective-permute-start(f32[4,192,128]{2,1,0:T(8,128)} %get-tuple-element.38), channel_id=1, source_target_pairs={{4,0},{8,4},{12,8},{16,12},{20,16},{24,20},{28,24},{5,1},{9,5},{13... | collective-permute-start | bytes 1179656 | tf_op jit(solution)/shard_map/ppermute | solution.py:19
  71.8 21.5 %collective-permute-start.2 = (bf16[8,4096]{1,0:T(8,128)(2,1)S(1)}, bf16[8,4096]{1,0:T(8,128)(2,1)S(1)}, u32[]{:S(2)}, u32[]{:S(2)}) collective-permute-start(bf16[8,4096]{1,0:T(8,128)(2,1)S(1)} %collective-permute-done.1), channel_id=1, source_target_pairs={{0,4},{4,8},{8,12},{12,16},{16,20},{20,24},{24,28},{1,5},{5,9},{9,... | collective-permute-start | bytes 196616 | tf_op jit(solution)/shard_map/ppermute | solution.py:19
  78.5 33.8 %collective-permute-start.8 = (f32[4,128,128]{2,1,0:T(8,128)}, f32[4,128,128]{2,1,0:T(8,128)S(1)}, u32[]{:S(2)}, u32[]{:S(2)}) collective-permute-start(f32[4,128,128]{2,1,0:T(8,128)} %get-tuple-element.39), channel_id=1, source_target_pairs={{4,0},{8,4},{12,8},{16,12},{20,16},{24,20},{28,24},{5,1},{9,5},{13... | collective-permute-start | bytes 786440 | tf_op jit(solution)/shard_map/ppermute | solution.py:19
  93.3 0.6 copy-start.7
  108.1 22.8 %collective-permute-start.3 = (f32[4,128,128]{2,1,0:T(8,128)}, f32[4,128,128]{2,1,0:T(8,128)S(1)}, u32[]{:S(2)}, u32[]{:S(2)}) collective-permute-start(f32[4,128,128]{2,1,0:T(8,128)} %get-tuple-element.27), channel_id=1, source_target_pairs={{0,4},{4,8},{8,12},{12,16},{16,20},{20,24},{24,28},{1,5},{5,9},{9,... | collective-permute-start | bytes 786440 | tf_op jit(solution)/shard_map/ppermute | solution.py:19
  112.3 0.7 copy-start.2
  112.3 0.8 copy-start.1
  130.8 0.7 copy-start.3
  131.5 4.9 %copy-start.5 = (f32[4,128,128]{2,1,0:T(8,128)S(1)}, f32[4,128,128]{2,1,0:T(8,128)}, u32[]{:S(2)}) copy-start(f32[4,128,128]{2,1,0:T(8,128)} %get-tuple-element.42) | copy-start | bytes 786436
Sparse Core Ops, SparseCore 0:
  130.9 74.3 all-reduce.2

commit v2 on v1

--- a/solution.py
+++ b/solution.py
@@ -7,7 +7,8 @@
 from jax.sharding import PartitionSpec as P
 
 F32 = jnp.float32
-UNROLL = 4
+SHIFT = 2
+UNROLL = 1 << SHIFT
 LANES = 128
 SUB = 8
 BLOCK = LANES * SUB
@@ -22,27 +23,6 @@
 def passed_along(array, axis, by):
     count = lax.axis_size(axis)
     return lax.ppermute(array, axis, [(i, (i + by) % count) for i in range(count)])
-
-
-def doc_meta(lengths, base, rows):
-    starts = jnp.cumsum(lengths) - lengths
-    places = base + jnp.arange(rows + 16, dtype=jnp.int32)
-    far = jnp.int32(1 << 30)
-    gaps = places[:, None] - starts[None, :]
-    age = jnp.min(jnp.where(gaps >= 0, gaps, far), axis=1)
-    keep = (age > 0).astype(jnp.int32)
-    positions = jnp.arange(rows, dtype=jnp.int32)
-    fresh = age[:rows] == 0
-    first = jnp.min(jnp.where(fresh, positions, rows))
-    last = jnp.max(jnp.where(fresh, positions, -1))
-    through = first == rows
-    u = UNROLL
-    front_hi = (first + u - 1) // u
-    main_lo = jnp.where(through, 0, first // u)
-    main_hi = jnp.where(through, rows // u, (last + u - 1) // u)
-    tail_lo = jnp.maximum(last, 0) // u
-    bounds = jnp.stack([front_hi, main_lo, main_hi, tail_lo, last, age[0]]).astype(jnp.int32)
-    return jnp.concatenate([bounds, jnp.zeros((2,), jnp.int32), keep]), through.astype(F32)
 
 
 HEAD = 8
@@ -149,7 +129,7 @@
             now = at(xs, t + 8)
             seen = [now] + [w * keep for w in window]
             q, k, v = [
-                total_of([at(taps, i * taps_count + j) * seen[j] for j in range(taps_count)])
+                total_of([taps[i * taps_count + j] * seen[j] for j in range(taps_count)])
                 for i in range(3)
             ]
             put(qs, t, q)
@@ -185,7 +165,7 @@
 
 
 def backward_kernel(
-    rows, modes, meta, up, qs, ks, vs, gs, longs, state, dtab, resid,
+    rows, modes, meta, up, qs, ks, vs, gs, longs, state, dtab, resid, after,
     dq, dl, dg, begin, sums, rim, ups,
 ):
     scatter_rows(up, ups, rows, 0)
@@ -222,8 +202,8 @@
 
 
 def finish_kernel(
-    rows, modes, taps_count, meta, xs, ks, vs, gs, dq, dl, dg, rim, state, sums, taps, dtab, resid,
-    out, tap_out, sums_out, dks, dvs, backs,
+    rows, modes, taps_count, group, meta, xs, ks, vs, gs, dq, dl, dg, rim, state, sums, taps, dtab, resid, after,
+    out, tap_out, dks, dvs, backs,
 ):
     def copy(g, _):
         for u in range(8):
@@ -238,12 +218,21 @@
         lambda t: jnp.where(t >= last, 1.0, 0.0).astype(F32),
         lambda t, y: put(dks, t, y),
     )
+    lane = lax.broadcasted_iota(jnp.int32, (SUB, LANES), 1)
+    groups = LANES // group
+    filter_tile = jnp.zeros((SUB, LANES), F32)
     for m in range(modes):
-        put(sums_out, m, totals[m])
+        part, step = totals[m], 1
+        while step < group:
+            part = part + pltpu.roll(part, LANES - step, 1)
+            step *= 2
+        moved = jnp.take_along_axis(part, lane % groups * group, axis=1)
+        filter_tile = jnp.where(lane // groups == m, moved, filter_tile)
+    tap_out[3 * taps_count] = filter_tile
 
     def spread(pending, grads, keep):
         parts = [
-            total_of([at(taps, i * taps_count + j) * grads[i] for i in range(3)])
+            total_of([taps[i * taps_count + j] * grads[i] for i in range(3)])
             for j in range(taps_count)
         ]
         done = pending[0] + parts[0]
@@ -296,7 +285,117 @@
 
     _, acc = lax.fori_loop(0, rows // 2, ascend, (window, zeros))
     for n in range(3 * taps_count):
-        put(tap_out, n, acc[n])
+        tap_out[n] = acc[n]
+
+
+def prepare_kernel(rows, blocks, lengths, rates, resids, meta_new, meta_old, dtab, resid):
+    base = lax.axis_index("ctx") * rows
+    reach = rows + 16
+    for which, meta in enumerate((meta_new, meta_old)):
+
+        def fill(i, _):
+            for u in range(8):
+                meta[i * 8 + u] = 1
+            return 0
+
+        lax.fori_loop(0, (HEAD + reach) // 8, fill, 0)
+
+        def document(i, carry):
+            offset, first, last, begin = carry
+            inside = jnp.logical_and(offset >= 0, offset < reach)
+            meta[jnp.where(inside, HEAD + offset, 7)] = 0
+            first = jnp.where(offset >= 0, jnp.minimum(first, offset), first)
+            last = jnp.where(jnp.logical_and(offset >= 0, offset < rows), offset, last)
+            begin = jnp.where(offset <= 0, offset, begin)
+            return offset + lengths[which, i], first, last, begin
+
+        start = (-base, jnp.int32(rows), jnp.int32(-1), jnp.int32(0))
+        _, first, last, begin = lax.fori_loop(0, lengths.shape[1], document, start)
+        through = first == rows
+        meta[0] = lax.shift_right_logical(first + (UNROLL - 1), SHIFT)
+        meta[1] = jnp.where(through, 0, lax.shift_right_logical(first, SHIFT))
+        meta[2] = jnp.where(through, rows // UNROLL, lax.shift_right_logical(last + (UNROLL - 1), SHIFT))
+        meta[3] = lax.shift_right_logical(jnp.maximum(last, 0), SHIFT)
+        meta[4] = last
+        meta[5] = -begin
+        meta[6] = jnp.where(through, 1, 0)
+    modes, filters = rates.shape
+    group = blocks * BLOCK // filters
+    lane = lax.broadcasted_iota(jnp.int32, (modes, LANES), 1) // group
+    zeros = jnp.zeros((modes * SUB, LANES), F32)
+    for b in range(blocks):
+        dtab[b, 0 : modes * SUB, :] = zeros
+        for c in range(SUB):
+            low = (b * SUB + c) * (LANES // group)
+            tile, place = low // LANES * LANES, low % LANES
+            for source, target, offset in ((rates, dtab, modes * SUB), (resids, resid, 0)):
+                wide = jnp.take_along_axis(source[:, tile : tile + LANES], lane + place, axis=1)
+                if target is dtab:
+                    wide = jnp.exp(-wide)
+                for h in range(0, modes, 8):
+                    target[b, pl.ds(offset + h * SUB + c, 8, stride=SUB), :] = wide[h : h + 8]
+
+
+def sum_kernel(count, chunk, own, out, inbox, send, arrive, share, gather):
+    me = lax.axis_index("ctx")
+    mine = pl.ds(me * chunk, chunk)
+    mesh_ids = pl.DeviceIdType.MESH
+
+    def peer_of(d):
+        return lax.rem(me + d + 1, count)
+
+    barrier = pltpu.get_barrier_semaphore()
+
+    def greet(d, _):
+        pl.semaphore_signal(barrier, inc=1, device_id={"ctx": peer_of(d)}, device_id_type=mesh_ids)
+        return 0
+
+    lax.fori_loop(0, count - 1, greet, 0)
+    pl.semaphore_wait(barrier, count - 1)
+
+    def piece(d):
+        peer = peer_of(d)
+        return pltpu.make_async_remote_copy(
+            src_ref=own.at[pl.ds(peer * chunk, chunk)], dst_ref=inbox.at[d],
+            send_sem=send.at[d], recv_sem=arrive.at[d],
+            device_id={"ctx": peer}, device_id_type=mesh_ids,
+        )
+
+    def result(d):
+        return pltpu.make_async_remote_copy(
+            src_ref=out.at[mine], dst_ref=out.at[mine],
+            send_sem=share.at[d], recv_sem=gather.at[d],
+            device_id={"ctx": peer_of(d)}, device_id_type=mesh_ids,
+        )
+
+    def landed(d):
+        sender = lax.rem(me - d - 1 + count, count)
+        theirs = pl.ds(sender * chunk, chunk)
+        return pltpu.make_async_remote_copy(
+            src_ref=out.at[mine], dst_ref=out.at[theirs],
+            send_sem=share.at[d], recv_sem=gather.at[d],
+            device_id={"ctx": peer_of(d)}, device_id_type=mesh_ids,
+        )
+
+    def loop(action):
+        def body(d, _):
+            action(d)
+            return 0
+
+        lax.fori_loop(0, count - 1, body, 0)
+
+    loop(lambda d: piece(d).start())
+    out[mine] = own[mine]
+
+    def collect(d):
+        piece(d).wait_recv()
+        out[mine] = out[mine] + inbox[d]
+
+    loop(collect)
+    loop(lambda d: result(d).start())
+    loop(lambda d: piece(d).wait_send())
+    loop(lambda d: landed(d).wait_recv())
+    loop(lambda d: result(d).wait_send())
 
 
 def on_device(section_out, stash, grad_out, taps, residues, decays, doc_lengths):
@@ -308,47 +407,56 @@
     blocks = width // BLOCK
     ctx_size = lax.axis_size("ctx")
     pipe_size = lax.axis_size("pipe")
-    base = lax.axis_index("ctx") * rows
     span = rows * ctx_size // 16 // rows + 1
     depth = (span - 1).bit_length()
 
+    smem = pl.BlockSpec(memory_space=pltpu.SMEM)
+    anywhere = pl.BlockSpec(memory_space=pl.ANY)
+    tokens = pl.BlockSpec((rows, BLOCK), lambda b: (0, b))
+    edge = pl.BlockSpec((8, BLOCK), lambda b: (0, b))
+
+    def major(count):
+        return pl.BlockSpec((None, count * SUB, LANES), lambda b: (b, 0, 0))
+
+    def shaped(count):
+        return jax.ShapeDtypeStruct((blocks, count * SUB, LANES), F32)
+
+    def scratch(count):
+        return pltpu.VMEM((count * SUB, LANES), F32)
+
+    def cost(ops, count):
+        return pl.CostEstimate(flops=ops * rows * width, bytes_accessed=4 * count * rows * width, transcendentals=0)
+
+    wide = jax.ShapeDtypeStruct((rows, width), jnp.bfloat16)
+    tail = [
+        pl.BlockSpec((branches * taps_count, SUB, LANES), lambda b: (0, b, 0)),
+        major(2 * modes),
+        major(modes),
+    ]
+    rim_old = from_behind(stashed[rows - 8 :], "ctx", 1)
+    rim_new = lax.ppermute(
+        section_out[0, rows - 8 :],
+        ("ctx", "pipe"),
+        [
+            (c * pipe_size + p, (c + 1) * pipe_size + (p + 1) % pipe_size)
+            for c in range(ctx_size - 1)
+            for p in range(pipe_size)
+        ],
+    )
     upstream = passed_along(grad_out, "pipe", -1)[0]
     incoming = passed_along(section_out, "pipe", 1)[0]
-    rim_old = from_behind(stashed[rows - 8 :], "ctx", 1)
-    rim_new = from_behind(passed_along(section_out[0, rows - 8 :], "pipe", 1), "ctx", 1)
-
-    meta_new, through_new = doc_meta(doc_lengths[0], base, rows)
-    meta_old, through_old = doc_meta(doc_lengths[1], base, rows)
-
-    def expand(small):
-        wide = jnp.broadcast_to(small[:, :, None], (modes, filters, group)).reshape(modes, blocks, SUB, LANES)
-        return jnp.swapaxes(wide, 0, 1).reshape(blocks, modes * SUB, LANES)
-
-    rates = expand(decays[0])
-    resid = expand(residues[0])
-    decay = jnp.exp(-rates)
-    dtab = jnp.concatenate([jnp.zeros_like(decay), decay], axis=1)
-    tapped = jnp.swapaxes(taps[0].reshape(branches * taps_count, blocks, SUB, LANES), 0, 1)
-    tapped = tapped.reshape(blocks, branches * taps_count * SUB, LANES)
-
-    smem = pl.BlockSpec(memory_space=pltpu.SMEM)
-    tokens = pl.BlockSpec((rows, BLOCK), lambda b: (0, b))
-    edge = pl.BlockSpec((8, BLOCK), lambda b: (0, b))
-
-    def major(count):
-        return pl.BlockSpec((None, count * SUB, LANES), lambda b: (b, 0, 0))
-
-    def shaped(count):
-        return jax.ShapeDtypeStruct((blocks, count * SUB, LANES), F32)
-
-    def scratch(count):
-        return pltpu.VMEM((count * SUB, LANES), F32)
-
-    def cost(ops, count):
-        return pl.CostEstimate(flops=ops * rows * width, bytes_accessed=4 * count * rows * width, transcendentals=0)
-
-    wide = jax.ShapeDtypeStruct((rows, width), jnp.bfloat16)
-    tail = [major(branches * taps_count), major(2 * modes), major(modes)]
+    whole = pl.BlockSpec(memory_space=pltpu.VMEM)
+    notes = jax.ShapeDtypeStruct((HEAD + rows + 16,), jnp.int32)
+    meta_new, meta_old, dtab, resid = pl.pallas_call(
+        functools.partial(prepare_kernel, rows, blocks),
+        in_specs=[smem, whole, whole],
+        out_specs=[smem, smem, whole, whole],
+        out_shape=[notes, notes, shaped(2 * modes), shaped(modes)],
+        name="prepare",
+    )(doc_lengths, decays[0], residues[0])
+    tapped = taps[0].reshape(branches * taps_count, blocks * SUB, LANES)
+    through_new, through_old = meta_new[6].astype(F32), meta_old[6].astype(F32)
+    decay = dtab[:, modes * SUB :]
 
     def link(earlier, later):
         return (earlier[0] * later[0], later[0] * earlier[1] + later[1])
@@ -356,7 +464,7 @@
     def nearby(through, summary, sign):
         if depth == 0:
             return from_behind(summary, "ctx", sign)
-        current = (through * jnp.exp(-rates * rows), summary)
+        current = (through * decay**rows, summary)
         for j in range(depth + 1):
             reach = 1 if j == 0 else 2 ** (j - 1)
             moved = from_behind(current, "ctx", sign * reach)
@@ -389,21 +497,18 @@
     dq, dl, dg, begin, sums, rim = pl.pallas_call(
         functools.partial(backward_kernel, rows, modes),
         grid=(blocks,),
-        in_specs=[smem, tokens] + [major(rows)] * 5 + [major(modes)] + tail[1:],
+        in_specs=[smem, tokens] + [major(rows)] * 5 + [major(modes)] + tail[1:] + [anywhere],
         out_specs=[major(rows)] * 3 + [major(modes)] * 2 + [major(24)],
         out_shape=[shaped(rows)] * 3 + [shaped(modes)] * 2 + [shaped(24)],
         scratch_shapes=[scratch(rows)],
         cost_estimate=cost(120, 8),
         name="backward_main",
-    )(meta_old, upstream, qs, ks, vs, gs, longs, state_old, dtab, resid)
+    )(meta_old, upstream, qs, ks, vs, gs, longs, state_old, dtab, resid, end_new)
     later = nearby(through_old, begin, -1)
     if depth > 0:
-        reach = (rows - jnp.arange(8, dtype=F32))[None, :, None, None, None]
         spread = (blocks, modes, SUB, LANES)
-        extra = jnp.sum(
-            (resid * later).reshape(spread)[:, None]
-            * jnp.exp(-rates.reshape(spread)[:, None] * jnp.swapaxes(reach, 2, 2)),
-            axis=2,
+        extra = jnp.stack(
+            [jnp.sum((resid * later * decay ** (rows - r)).reshape(spread), axis=1) for r in range(8)], axis=1
         ).reshape(blocks, 8 * SUB, LANES) * through_old
         head = 8 * SUB
         rim = rim + jnp.concatenate(
@@ -422,25 +527,38 @@
         name="mixed",
     )(meta_new, qn, gn, longn, state_new, dtab, resid)
 
-    back, tap_term, totals = pl.pallas_call(
-        functools.partial(finish_kernel, rows, modes, taps_count),
+    slots = branches * taps_count + 1
+    back, partial = pl.pallas_call(
+        functools.partial(finish_kernel, rows, modes, taps_count, group),
         grid=(blocks,),
-        in_specs=[smem, major(rows + 8)] + [major(rows)] * 6 + [major(24)] + [major(modes)] * 2 + tail,
-        out_specs=[tokens, major(branches * taps_count), major(modes)],
-        out_shape=[wide, shaped(branches * taps_count), shaped(modes)],
+        in_specs=[smem, major(rows + 8)] + [major(rows)] * 6 + [major(24)] + [major(modes)] * 2 + tail + [anywhere],
+        out_specs=[tokens, pl.BlockSpec((slots, SUB, LANES), lambda b: (0, b, 0))],
+        out_shape=[wide, jax.ShapeDtypeStruct((slots, blocks * SUB, LANES), F32)],
         scratch_shapes=[scratch(rows)] * 3,
         cost_estimate=cost(150, 8),
         name="finish",
-    )(meta_old, xs, ks, vs, gs, dq, dl, dg, rim_in, later, sums, tapped, dtab, resid)
-
-    filter_term = jnp.sum(
-        jnp.swapaxes(totals.reshape(blocks, modes, SUB, LANES), 0, 1).reshape(modes, filters, group), axis=2
-    )
-    tap_term = jnp.swapaxes(tap_term.reshape(blocks, branches * taps_count, SUB, LANES), 0, 1).reshape(
-        branches, taps_count, width
-    )
-    summed = lax.psum((filter_term, tap_term), "ctx")
-    return (mixed[None], back[None], summed[0][None], summed[1][None])
+    )(meta_old, xs, ks, vs, gs, dq, dl, dg, rim_in, later, sums, tapped, dtab, resid, mixed)
+
+    tiles = slots * blocks
+    chunk = -(-tiles // ctx_size)
+    partial = partial.reshape(tiles, SUB, LANES)
+    if chunk * ctx_size > tiles:
+        partial = jnp.pad(partial, ((0, chunk * ctx_size - tiles), (0, 0), (0, 0)))
+    hops = ctx_size - 1
+    summed = pl.pallas_call(
+        functools.partial(sum_kernel, ctx_size, chunk),
+        in_specs=[whole],
+        out_specs=whole,
+        out_shape=jax.ShapeDtypeStruct(partial.shape, F32),
+        scratch_shapes=[pltpu.VMEM((hops, chunk, SUB, LANES), F32)] + [pltpu.SemaphoreType.DMA((hops,))] * 4,
+        compiler_params=pltpu.CompilerParams(collective_id=0, has_side_effects=True),
+        name="window_sum",
+    )(partial)
+    cut = branches * taps_count * blocks
+    tap_term = summed[:cut].reshape(branches, taps_count, width)
+    filter_term = summed[cut:tiles].reshape(blocks, SUB, modes, LANES // group)
+    filter_term = filter_term.transpose(2, 0, 1, 3).reshape(modes, filters)
+    return (mixed[None], back[None], filter_term[None], tap_term[None])
 
 
 def solution(mesh):

time: 213 us -> 142 us (0.67)
  blocking collectives: 36.5 us -> 0 us
  Pallas kernels: 61.9 us -> 89.7 us
  between operations: 24.8 us -> 0.81 us
  waiting for transfers between devices: 42.3 us -> 22.2 us
  local copies, waits for them, and re-layouts: 22.6 us -> 9.29 us
  other arithmetic: 4.47 us -> 0 us
  starting transfers between devices: 21.4 us -> 19.1 us
    psum x1 -> x0, blocking collectives: 36.5 us -> none  [on_device(): summed = lax.psum((filter_term, tap_term), 'ctx')]
    psum x1 -> x0, waiting for transfers between devices: 31.2 us -> none  [on_device(): summed = lax.psum((filter_term, tap_term), 'ctx')]
    pallas_call x1 -> x3, Pallas kernels: 15.9 us -> 44 us  [the longest x1 23.6 us: on_device(): pl.pallas_call(functools.partial(sum_kernel, ctx_size, chunk), in_specs=[...]
    ppermute x6 -> x5, waiting for transfers between devices: 11.1 us -> 17.5 us  [from_behind(): lax.ppermute(value, axis, [(source, source + steps) for source in range(i...]
    concatenate x3 -> x0, local copies, waits for them, and re-layouts: 5.69 us -> none  [the longest x2 3.88 us: doc_meta(): jnp.concatenate([bounds, jnp.zeros((2,), jnp.int32), keep])]
    ppermute x6 -> x5, starting transfers between devices: 19.9 us -> 14.7 us  [from_behind(): lax.ppermute(value, axis, [(source, source + steps) for source in range(i...]
    ppermute x0 -> x1, waiting for transfers between devices: none -> 4.66 us  [on_device(): lax.ppermute(section_out[0, rows - 8:], ('ctx', 'pipe'), [(c * pipe_size...]
    unnamed x27 -> x19, local copies, waits for them, and re-layouts: 5.56 us -> 4.89 us
  transfers between devices with their start and end apart: 10 -> 8, of which waited for: 3 -> 2; matrix products, arithmetic and copies ran while one was open for 10% -> 1% of each run, Pallas kernels for 29% -> 26%
where the time goes in v2:
time: 142 us; the launch traced here: 141 us
  Pallas kernels  89.7 us (63%)
  waiting for transfers between devices  22.2 us (16%)
  starting transfers between devices  19.1 us (13%)
  local copies, waits for them, and re-layouts  9.29 us (7%)
    pallas_call x2, Pallas kernels, on_device(): pl.pallas_call(functools.partial(forward_kernel, rows, modes, taps_count,...  28.8 us
    pallas_call x1, Pallas kernels, on_device(): pl.pallas_call(functools.partial(sum_kernel, ctx_size, chunk), in_specs=[...  23.6 us
    pallas_call x1, Pallas kernels, on_device(): pl.pallas_call(functools.partial(finish_kernel, rows, modes, taps_count,...  17.5 us
    ppermute x5, waiting for transfers between devices, from_behind(): lax.ppermute(value, axis, [(source, source + steps) for source in range(i...  17.5 us
    ppermute x5, starting transfers between devices, from_behind(): lax.ppermute(value, axis, [(source, source + steps) for source in range(i...  14.7 us
    pallas_call x1, Pallas kernels, on_device(): pl.pallas_call(functools.partial(backward_kernel, rows, modes), grid=(blo...  12.1 us
    unnamed x19, local copies, waits for them, and re-layouts  4.89 us
    pallas_call x1, Pallas kernels, on_device(): pl.pallas_call(functools.partial(mixed_kernel, rows, modes), grid=(blocks...  4.87 us
  transfers between devices with their start and end apart: 8, of which 2 were waited for; matrix products, arithmetic and copies ran while one was open for 1% of the time, Pallas kernels for 26%

profile of v2, /device:TPU:0, one launch (start us, length us, event | category | flops | bytes accessed | tf_op | source)
XLA Modules:
  0.0 141.1 jit_solution(11435531244281841533)
XLA Ops:
  0.6 2.5 %collective-permute-start.4 = (bf16[1,128,4096]{2,1,0:T(8,128)(2,1)}, bf16[1,128,4096]{2,1,0:T(8,128)(2,1)S(1)}, u32[]{:S(2)}, u32[]{:S(2)}) collective-permute-start(bf16[1,128,4096]{2,1,0:T(8,128)(2,1)} %param.9), channel_id=1, source_target_pairs={{0,3},{1,0},{2,1},{3,2},{4,7},{5,4},{6,5},{7,6},{8,11},{9,8},{10,9... | collective-permute-start | bytes 3145736 | tf_op jit(solution)/shard_map/ppermute | solution.py:25
  3.1 0.0 collective-permute-start
  3.1 0.8 slice_bitcast_fusion
  4.0 3.4 %collective-permute-start.3 = (bf16[8,4096]{1,0:T(8,128)(2,1)S(1)}, bf16[8,4096]{1,0:T(8,128)(2,1)S(1)}, u32[]{:S(2)}, u32[]{:S(2)}) collective-permute-start(bf16[8,4096]{1,0:T(8,128)(2,1)S(1)} %slice_bitcast_fusion), channel_id=1, source_target_pairs={{0,4},{4,8},{8,12},{12,16},{16,20},{20,24},{24,28},{1,5},{5,9},{9,... | collective-permute-start | bytes 196616 | tf_op jit(solution)/shard_map/ppermute | solution.py:20
  7.4 2.8 %prepare.1 = (s32[152]{0:T(256)}, s32[152]{0:T(256)}, f32[4,256,128]{2,1,0:T(8,128)}, f32[4,128,128]{2,1,0:T(8,128)}) custom-call(s32[2,24]{1,0:T(2,128)} %lengths.1, f32[16,256]{1,0:T(8,128)} %bitcast.27, f32[16,256]{1,0:T(8,128)} %bitcast.28), custom_call_target="tpu_custom_call" | custom-call | tf_op jit(solution)/shard_map/prepare/pallas_call | solution.py:450
  10.2 0.0 collective-permute-done.3.rim
  10.2 0.0 copy-start.7
  10.2 0.6 copy-done.7
  10.9 14.6 %forward_old.1 = (f32[4,1088,128]{2,1,0:T(8,128)}, f32[4,1024,128]{2,1,0:T(8,128)}, f32[4,1024,128]{2,1,0:T(8,128)}, f32[4,1024,128]{2,1,0:T(8,128)}, f32[4,1024...) custom-call(s32[152]{0:T(256)} %get-tuple-element.34.meta, bf16[128,4096]{1,0:T(8,128)(2,1)} %bitcast.20, ...), custom_call_target="tpu_custom_call" | custom-call | flops 57671680 | bytes 14680064 | tf_op jit(solution)/shard_map/forward_old/pallas_call | solution.py:474
  25.4 3.4 %collective-permute-start.5 = (f32[4,128,128]{2,1,0:T(8,128)}, f32[4,128,128]{2,1,0:T(8,128)S(1)}, u32[]{:S(2)}, u32[]{:S(2)}) collective-permute-start(f32[4,128,128]{2,1,0:T(8,128)} %get-tuple-element.41), channel_id=1, source_target_pairs={{0,4},{4,8},{8,12},{12,16},{16,20},{20,24},{24,28},{1,5},{5,9},{9,... | collective-permute-start | bytes 786440 | tf_op jit(solution)/shard_map/ppermute | solution.py:20
  28.8 0.8 slice_bitcast_fusion.1
  29.7 2.0 %collective-permute-start.1 = (bf16[8,4096]{1,0:T(8,128)(2,1)S(1)}, bf16[8,4096]{1,0:T(8,128)(2,1)S(1)}, u32[]{:S(2)}, u32[]{:S(2)}) collective-permute-start(bf16[8,4096]{1,0:T(8,128)(2,1)S(1)} %slice_bitcast_fusion.1), channel_id=1, source_target_pairs={{0,5},{1,6},{2,7},{3,4},{4,9},{5,10},{6,11},{7,8},{8,13},{9,14},{1... | collective-permute-start | bytes 196616 | tf_op jit(solution)/shard_map/ppermute | solution.py:437
  31.7 4.7 %collective-permute-done.1.rim = bf16[8,4096]{1,0:T(8,128)(2,1)S(1)} collective-permute-done((bf16[8,4096]{1,0:T(8,128)(2,1)S(1)}, bf16[8,4096]{1,0:T(8,128)(2,1)S(1)}, u32[]{:S(2)}, u32[]{:S(2)}) %collective-permute-start.1) | collective-permute-done | bytes 65568 | tf_op jit(solution)/shard_map/ppermute | solution.py:437
  36.3 0.0 copy-start.8
  36.3 0.0 collective-permute-done
  36.3 0.0 copy-start.1
  36.3 0.6 copy-done.8
  36.9 0.4 copy-done.1
  37.3 14.2 %forward_new.1 = (f32[4,1024,128]{2,1,0:T(8,128)}, f32[4,1024,128]{2,1,0:T(8,128)}, f32[4,1024,128]{2,1,0:T(8,128)}, f32[4,128,128]{2,1,0:T(8,128)}) custom-call(s32[152]{0:T(256)} %get-tuple-element.27.meta, bf16[128,4096]{1,0:T(8,128)(2,1)} %bitcast.22, bf16[8,4096]{1,0:T(8,128)(2,1)} %copy-done.8, f32[21,32,128]{2,1,0:T(8,128)} %bitcast.18, ...), custom_call_target="tpu_custom_call" | custom-call | flops 57671680 | bytes 8388608 | tf_op jit(solution)/shard_map/forward_new/pallas_call | solution.py:485
  51.5 0.0 collective-permute-done.5.state
  51.5 0.0 copy-start.4
  51.5 0.0 collective-permute-done.4
  51.5 0.0 copy-start
  51.6 0.7 copy-done.4
  52.2 0.4 copy-done
  52.6 0.0 copy-start.5
  52.6 12.1 %backward_main.1 = (f32[4,1024,128]{2,1,0:T(8,128)}, f32[4,1024,128]{2,1,0:T(8,128)}, f32[4,1024,128]{2,1,0:T(8,128)}, f32[4,128,128]{2,1,0:T(8,128)}, f32[4,128,128]{2,1,0:T(8,128)}, /*index=5*/f32[4,192,128]{2,1,0:T(8,128)}) custom-call(s32[152]{0:T(256)} %get-tuple-element.34.meta, bf16[128,4096]{1,0:T(8,128)(2,1)} %bitcast.21, ...), custom_call_target="tpu_custom_call" | custom-call | flops 62914560 | bytes 16777216 | tf_op jit(solution)/shard_map/backward_main/pallas_call | solution.py:497
  64.7 1.3 collective-permute-start.6
  66.0 0.0 copy-done.5
  66.0 5.3 %collective-permute-start.2 = (f32[4,128,128]{2,1,0:T(8,128)S(1)}, f32[4,128,128]{2,1,0:T(8,128)S(1)}, u32[]{:S(2)}, u32[]{:S(2)}) collective-permute-start(f32[4,128,128]{2,1,0:T(8,128)S(1)} %copy-done.5), channel_id=1, source_target_pairs={{0,4},{4,8},{8,12},{12,16},{16,20},{20,24},{24,28},{1,5},{5,9},{9,... | collective-permute-start | bytes 786440 | tf_op jit(solution)/shard_map/ppermute | solution.py:20
  71.3 1.3 collective-permute-start.7
  72.6 17.5 %collective-permute-done.2.state = f32[4,128,128]{2,1,0:T(8,128)S(1)} collective-permute-done((f32[4,128,128]{2,1,0:T(8,128)S(1)}, f32[4,128,128]{2,1,0:T(8,128)S(1)}, u32[]{:S(2)}, u32[]{:S(2)}) %collective-permute-start.2) | collective-permute-done | bytes 262176 | tf_op jit(solution)/shard_map/ppermute | solution.py:20
  90.0 0.0 copy-start.6
  90.0 0.7 copy-done.6
  90.8 4.9 %mixed.1.after = bf16[128,4096]{1,0:T(8,128)(2,1)} custom-call(s32[152]{0:T(256)} %get-tuple-element.27.meta, f32[4,1024,128]{2,1,0:T(8,128)} %get-tuple-element.30.qs, f32[4,1024,128]{2,1,0:T(8,128)} %get-tuple-element.31.gs, f32[4,1024,128]{2,1,0:T(8,128)} %get-tuple-element.32.longs, f32[4,128,128]{2,1,0:T(8,128)} %copy-done.6, ...), custom_call_target="tpu_custom_call" | custom-call | flops 15728640 | bytes 8388608 | tf_op jit(solution)/shard_map/mixed/pallas_call | solution.py:519
  95.6 0.0 collective-permute-done.7.state
  95.6 0.0 copy-start.3
  95.6 0.0 collective-permute-done.6.rim
  95.6 0.0 copy-start.2
  95.7 0.7 copy-done.3
  96.3 0.2 copy-done.2
  96.5 17.5 %finish.1 = (bf16[128,4096]{1,0:T(8,128)(2,1)}, f32[22,32,128]{2,1,0:T(8,128)}) custom-call(s32[152]{0:T(256)} %get-tuple-element.34.meta, f32[4,1088,128]{2,1,0:T(8,128)} %get-tuple-element.35.xs, f32[4,1024,128]{2,1,0:T(8,128)} %get-tuple-element.36.ks, f32[4,1024,128]{2,1,0:T(8,128)} %get-tuple-element.37.vs, f32[4,1024,128]{2,1,0:T(8,128)} %get-tuple-element.38.gs, ...), custom_call_target="tpu_custom_call" | custom-call | flops 78643200 | bytes 16777216 | tf_op jit(solution)/shard_map/finish/pallas_call | solution.py:531
  114.0 23.6 %window_sum.1 = f32[88,8,128]{2,1,0:T(8,128)} custom-call(f32[88,8,128]{2,1,0:T(8,128)} %bitcast.25), custom_call_target="tpu_custom_call" | custom-call | tf_op jit(solution)/shard_map/window_sum/pallas_call | solution.py:548
  137.7 0.7 slice.18
  138.4 1.7 %slice.19 = f32[84,8,128]{2,1,0:T(8,128)} slice(f32[88,8,128]{2,1,0:T(8,128)} %window_sum.1), slice={[0:84], [0:8], [0:128]} | slice | bytes 688128 | tf_op jit(solution)/shard_map/slice | solution.py:558
  140.1 0.2 reshape.16
  140.3 0.1 copy.13
  140.4 0.7 copy.14
Async XLA Ops:
  0.6 50.9 %collective-permute-start.4 = (bf16[1,128,4096]{2,1,0:T(8,128)(2,1)}, bf16[1,128,4096]{2,1,0:T(8,128)(2,1)S(1)}, u32[]{:S(2)}, u32[]{:S(2)}) collective-permute-start(bf16[1,128,4096]{2,1,0:T(8,128)(2,1)} %param.9), channel_id=1, source_target_pairs={{0,3},{1,0},{2,1},{3,2},{4,7},{5,4},{6,5},{7,6},{8,11},{9,8},{10,9... | collective-permute-start | bytes 3145736 | tf_op jit(solution)/shard_map/ppermute | solution.py:25
  3.1 33.2 %collective-permute-start = (bf16[1,128,4096]{2,1,0:T(8,128)(2,1)}, bf16[1,128,4096]{2,1,0:T(8,128)(2,1)S(1)}, u32[]{:S(2)}, u32[]{:S(2)}) collective-permute-start(bf16[1,128,4096]{2,1,0:T(8,128)(2,1)} %param.7), channel_id=1, source_target_pairs={{0,1},{1,2},{2,3},{3,0},{4,5},{5,6},{6,7},{7,4},{8,9},{9,10},{10,1... | collective-permute-start | bytes 3145736 | tf_op jit(solution)/shard_map/ppermute | solution.py:25
  4.0 6.3 %collective-permute-start.3 = (bf16[8,4096]{1,0:T(8,128)(2,1)S(1)}, bf16[8,4096]{1,0:T(8,128)(2,1)S(1)}, u32[]{:S(2)}, u32[]{:S(2)}) collective-permute-start(bf16[8,4096]{1,0:T(8,128)(2,1)S(1)} %slice_bitcast_fusion), channel_id=1, source_target_pairs={{0,4},{4,8},{8,12},{12,16},{16,20},{20,24},{24,28},{1,5},{5,9},{9,... | collective-permute-start | bytes 196616 | tf_op jit(solution)/shard_map/ppermute | solution.py:20
  10.2 0.6 copy-start.7
  25.4 26.1 %collective-permute-start.5 = (f32[4,128,128]{2,1,0:T(8,128)}, f32[4,128,128]{2,1,0:T(8,128)S(1)}, u32[]{:S(2)}, u32[]{:S(2)}) collective-permute-start(f32[4,128,128]{2,1,0:T(8,128)} %get-tuple-element.41), channel_id=1, source_target_pairs={{0,4},{4,8},{8,12},{12,16},{16,20},{20,24},{24,28},{1,5},{5,9},{9,... | collective-permute-start | bytes 786440 | tf_op jit(solution)/shard_map/ppermute | solution.py:20
  29.7 6.6 %collective-permute-start.1 = (bf16[8,4096]{1,0:T(8,128)(2,1)S(1)}, bf16[8,4096]{1,0:T(8,128)(2,1)S(1)}, u32[]{:S(2)}, u32[]{:S(2)}) collective-permute-start(bf16[8,4096]{1,0:T(8,128)(2,1)S(1)} %slice_bitcast_fusion.1), channel_id=1, source_target_pairs={{0,5},{1,6},{2,7},{3,4},{4,9},{5,10},{6,11},{7,8},{8,13},{9,14},{1... | collective-permute-start | bytes 196616 | tf_op jit(solution)/shard_map/ppermute | solution.py:437
  36.3 0.6 copy-start.8
  36.3 1.0 copy-start.1
  51.5 0.7 copy-start.4
  51.5 1.0 copy-start
  52.6 13.4 %copy-start.5 = (f32[4,128,128]{2,1,0:T(8,128)S(1)}, f32[4,128,128]{2,1,0:T(8,128)}, u32[]{:S(2)}) copy-start(f32[4,128,128]{2,1,0:T(8,128)} %get-tuple-element.33.after) | copy-start | bytes 786436
  64.7 31.0 %collective-permute-start.6 = (f32[4,192,128]{2,1,0:T(8,128)}, f32[4,192,128]{2,1,0:T(8,128)S(1)}, u32[]{:S(2)}, u32[]{:S(2)}) collective-permute-start(f32[4,192,128]{2,1,0:T(8,128)} %get-tuple-element.45), channel_id=1, source_target_pairs={{4,0},{8,4},{12,8},{16,12},{20,16},{24,20},{28,24},{5,1},{9,5},{13... | collective-permute-start | bytes 1179656 | tf_op jit(solution)/shard_map/ppermute | solution.py:20
  66.0 24.1 %collective-permute-start.2 = (f32[4,128,128]{2,1,0:T(8,128)S(1)}, f32[4,128,128]{2,1,0:T(8,128)S(1)}, u32[]{:S(2)}, u32[]{:S(2)}) collective-permute-start(f32[4,128,128]{2,1,0:T(8,128)S(1)} %copy-done.5), channel_id=1, source_target_pairs={{0,4},{4,8},{8,12},{12,16},{16,20},{20,24},{24,28},{1,5},{5,9},{9,... | collective-permute-start | bytes 786440 | tf_op jit(solution)/shard_map/ppermute | solution.py:20
  71.3 24.4 %collective-permute-start.7 = (f32[4,128,128]{2,1,0:T(8,128)}, f32[4,128,128]{2,1,0:T(8,128)S(1)}, u32[]{:S(2)}, u32[]{:S(2)}) collective-permute-start(f32[4,128,128]{2,1,0:T(8,128)} %get-tuple-element.46), channel_id=1, source_target_pairs={{4,0},{8,4},{12,8},{16,12},{20,16},{24,20},{28,24},{5,1},{9,5},{13... | collective-permute-start | bytes 786440 | tf_op jit(solution)/shard_map/ppermute | solution.py:20
  90.0 0.7 copy-start.6
  95.6 0.7 copy-start.3
  95.6 0.8 copy-start.2

commit v3 on v2

--- a/solution.py
+++ b/solution.py
@@ -5,6 +5,7 @@
 from jax.experimental import pallas as pl
 from jax.experimental.pallas import tpu as pltpu
 from jax.sharding import PartitionSpec as P
+
 
 F32 = jnp.float32
 SHIFT = 2
@@ -166,7 +167,7 @@
 
 def backward_kernel(
     rows, modes, meta, up, qs, ks, vs, gs, longs, state, dtab, resid, after,
-    dq, dl, dg, begin, sums, rim, ups,
+    dq, dl, dg, turn, sums, ups,
 ):
     scatter_rows(up, ups, rows, 0)
 
@@ -192,17 +193,17 @@
         lambda t, y: put(dg, t, y),
     )
     for m in range(modes):
-        put(begin, m, states[m])
+        put(turn, m, states[m])
         put(sums, m, totals[m])
     for t in range(8):
         value = at(dg, t)
-        put(rim, t, at(dq, t))
-        put(rim, 8 + t, value * at(vs, t))
-        put(rim, 16 + t, value * at(ks, t))
+        put(turn, modes + t, at(dq, t))
+        put(turn, modes + 8 + t, value * at(vs, t))
+        put(turn, modes + 16 + t, value * at(ks, t))
 
 
 def finish_kernel(
-    rows, modes, taps_count, group, meta, xs, ks, vs, gs, dq, dl, dg, rim, state, sums, taps, dtab, resid, after,
+    rows, modes, taps_count, group, meta, xs, ks, vs, gs, dq, dl, dg, turn, sums, taps, dtab, resid, after,
     out, tap_out, dks, dvs, backs,
 ):
     def copy(g, _):
@@ -213,7 +214,7 @@
     lax.fori_loop(0, rows // 8, copy, 0)
     last = meta[4]
     _, totals = scan_backward(
-        meta, dl, gs, dtab, resid, meta[3], rows // UNROLL, load_states(state, modes),
+        meta, dl, gs, dtab, resid, meta[3], rows // UNROLL, load_states(turn, modes),
         load_states(sums, modes),
         lambda t: jnp.where(t >= last, 1.0, 0.0).astype(F32),
         lambda t, y: put(dks, t, y),
@@ -244,7 +245,7 @@
 
     pending = tuple(jnp.zeros((SUB, LANES), F32) for _ in range(taps_count - 1))
     for r in reversed(range(taps_count - 1)):
-        grads = [at(rim, i * 8 + r) for i in range(3)]
+        grads = [at(turn, modes + i * 8 + r) for i in range(3)]
         _, pending = spread(pending, grads, meta[HEAD + rows + r].astype(F32))
 
     def descend(i, pending):
@@ -494,18 +495,21 @@
     )(meta_new, incoming, rim_new, tapped, dtab, resid)
     state_new = nearby(through_new, end_new, 1)
 
-    dq, dl, dg, begin, sums, rim = pl.pallas_call(
+    dq, dl, dg, turn, sums = pl.pallas_call(
         functools.partial(backward_kernel, rows, modes),
         grid=(blocks,),
         in_specs=[smem, tokens] + [major(rows)] * 5 + [major(modes)] + tail[1:] + [anywhere],
-        out_specs=[major(rows)] * 3 + [major(modes)] * 2 + [major(24)],
-        out_shape=[shaped(rows)] * 3 + [shaped(modes)] * 2 + [shaped(24)],
+        out_specs=[major(rows)] * 3 + [major(modes + 24), major(modes)],
+        out_shape=[shaped(rows)] * 3 + [shaped(modes + 24), shaped(modes)],
         scratch_shapes=[scratch(rows)],
         cost_estimate=cost(120, 8),
         name="backward_main",
-    )(meta_old, upstream, qs, ks, vs, gs, longs, state_old, dtab, resid, end_new)
-    later = nearby(through_old, begin, -1)
-    if depth > 0:
+    )(meta_old, upstream, qs, ks, vs, gs, longs, state_old, dtab, resid, state_new)
+    if depth == 0:
+        turn_in = from_behind(turn, "ctx", -1)
+    else:
+        later = nearby(through_old, turn[:, : modes * SUB], -1)
+        rim = turn[:, modes * SUB :]
         spread = (blocks, modes, SUB, LANES)
         extra = jnp.stack(
             [jnp.sum((resid * later * decay ** (rows - r)).reshape(spread), axis=1) for r in range(8)], axis=1
@@ -514,7 +518,7 @@
         rim = rim + jnp.concatenate(
             [jnp.zeros_like(extra), extra * vs[:, :head], extra * ks[:, :head]], axis=1
         )
-    rim_in = from_behind(rim, "ctx", -1)
+        turn_in = jnp.concatenate([later, from_behind(rim, "ctx", -1)], axis=1)
 
     mixed = pl.pallas_call(
         functools.partial(mixed_kernel, rows, modes),
@@ -531,13 +535,13 @@
     back, partial = pl.pallas_call(
         functools.partial(finish_kernel, rows, modes, taps_count, group),
         grid=(blocks,),
-        in_specs=[smem, major(rows + 8)] + [major(rows)] * 6 + [major(24)] + [major(modes)] * 2 + tail + [anywhere],
+        in_specs=[smem, major(rows + 8)] + [major(rows)] * 6 + [major(modes + 24), major(modes)] + tail + [anywhere],
         out_specs=[tokens, pl.BlockSpec((slots, SUB, LANES), lambda b: (0, b, 0))],
         out_shape=[wide, jax.ShapeDtypeStruct((slots, blocks * SUB, LANES), F32)],
         scratch_shapes=[scratch(rows)] * 3,
         cost_estimate=cost(150, 8),
         name="finish",
-    )(meta_old, xs, ks, vs, gs, dq, dl, dg, rim_in, later, sums, tapped, dtab, resid, mixed)
+    )(meta_old, xs, ks, vs, gs, dq, dl, dg, turn_in, sums, tapped, dtab, resid, mixed)
 
     tiles = slots * blocks
     chunk = -(-tiles // ctx_size)
@@ -577,6 +581,7 @@
         P("pipe", None, None),
         P("pipe", None, None, None),
     )
+
     return jax.shard_map(
         on_device, mesh=mesh, in_specs=in_specs, out_specs=out_specs, check_vma=False
     )

time: 142 us -> 136 us (0.958)
  starting transfers between devices: 19.1 us -> 14.9 us
  waiting for transfers between devices: 22.2 us -> 20.5 us
    ppermute x5 -> x4, starting transfers between devices: 14.7 us -> 9.9 us  [from_behind(): lax.ppermute(value, axis, [(source, source + steps) for source in range(i...]
    ppermute x1, waiting for transfers between devices: 4.66 us -> 0.01 us  [on_device(): lax.ppermute(section_out[0, rows - 8:], ('ctx', 'pipe'), [(c * pipe_size...]
    ppermute x5 -> x4, waiting for transfers between devices: 17.5 us -> 20.5 us  [from_behind(): lax.ppermute(value, axis, [(source, source + steps) for source in range(i...]
    unnamed x19 -> x15, local copies, waits for them, and re-layouts: 4.89 us -> 3.86 us
  transfers between devices with their start and end apart: 8 -> 7, of which waited for: 2 -> 2; matrix products, arithmetic and copies ran while one was open for 1% -> 1% of each run, Pallas kernels for 26% -> 27%
where the time goes in v3:
time: 136 us; the launch traced here: 135 us
  Pallas kernels  90.6 us (67%)
  waiting for transfers between devices  20.5 us (15%)
  starting transfers between devices  14.9 us (11%)
  local copies, waits for them, and re-layouts  8.26 us (6%)
    pallas_call x2, Pallas kernels, on_device(): pl.pallas_call(functools.partial(forward_kernel, rows, modes, taps_count,...  28.8 us
    pallas_call x1, Pallas kernels, on_device(): pl.pallas_call(functools.partial(sum_kernel, ctx_size, chunk), in_specs=[...  24.2 us
    ppermute x4, waiting for transfers between devices, from_behind(): lax.ppermute(value, axis, [(source, source + steps) for source in range(i...  20.5 us
    pallas_call x1, Pallas kernels, on_device(): pl.pallas_call(functools.partial(finish_kernel, rows, modes, taps_count,...  18.3 us
    pallas_call x1, Pallas kernels, on_device(): pl.pallas_call(functools.partial(backward_kernel, rows, modes), grid=(blo...  11.7 us
    ppermute x4, starting transfers between devices, from_behind(): lax.ppermute(value, axis, [(source, source + steps) for source in range(i...  9.9 us
    pallas_call x1, Pallas kernels, on_device(): pl.pallas_call(functools.partial(mixed_kernel, rows, modes), grid=(blocks...  4.89 us
    unnamed x15, local copies, waits for them, and re-layouts  3.86 us
  transfers between devices with their start and end apart: 7, of which 2 were waited for; matrix products, arithmetic and copies ran while one was open for 1% of the time, Pallas kernels for 27%

profile of v3, /device:TPU:0, one launch (start us, length us, event | category | flops | bytes accessed | tf_op | source)
XLA Modules:
  0.0 135.1 jit_solution(1926439591490332050)
XLA Ops:
  0.6 0.5 collective-permute-start
  1.2 0.8 slice_bitcast_fusion
  2.0 4.4 %collective-permute-start.3 = (bf16[8,4096]{1,0:T(8,128)(2,1)S(1)}, bf16[8,4096]{1,0:T(8,128)(2,1)S(1)}, u32[]{:S(2)}, u32[]{:S(2)}) collective-permute-start(bf16[8,4096]{1,0:T(8,128)(2,1)S(1)} %slice_bitcast_fusion), channel_id=1, source_target_pairs={{0,4},{4,8},{8,12},{12,16},{16,20},{20,24},{24,28},{1,5},{5,9},{9,... | collective-permute-start | bytes 196616 | tf_op jit(solution)/shard_map/ppermute | solution.py:21
  6.4 1.5 %collective-permute-start.4 = (bf16[1,128,4096]{2,1,0:T(8,128)(2,1)}, bf16[1,128,4096]{2,1,0:T(8,128)(2,1)S(1)}, u32[]{:S(2)}, u32[]{:S(2)}) collective-permute-start(bf16[1,128,4096]{2,1,0:T(8,128)(2,1)} %param.9), channel_id=1, source_target_pairs={{0,3},{1,0},{2,1},{3,2},{4,7},{5,4},{6,5},{7,6},{8,11},{9,8},{10,9... | collective-permute-start | bytes 3145736 | tf_op jit(solution)/shard_map/ppermute | solution.py:26
  7.9 0.8 slice_bitcast_fusion.1
  8.8 3.0 %collective-permute-start.1 = (bf16[8,4096]{1,0:T(8,128)(2,1)S(1)}, bf16[8,4096]{1,0:T(8,128)(2,1)S(1)}, u32[]{:S(2)}, u32[]{:S(2)}) collective-permute-start(bf16[8,4096]{1,0:T(8,128)(2,1)S(1)} %slice_bitcast_fusion.1), channel_id=1, source_target_pairs={{0,5},{1,6},{2,7},{3,4},{4,9},{5,10},{6,11},{7,8},{8,13},{9,14},{1... | collective-permute-start | bytes 196616 | tf_op jit(solution)/shard_map/ppermute | solution.py:438
  11.7 2.8 %prepare.1 = (s32[152]{0:T(256)}, s32[152]{0:T(256)}, f32[4,256,128]{2,1,0:T(8,128)}, f32[4,128,128]{2,1,0:T(8,128)}) custom-call(s32[2,24]{1,0:T(2,128)} %lengths.1, f32[16,256]{1,0:T(8,128)} %bitcast.27, f32[16,256]{1,0:T(8,128)} %bitcast.28), custom_call_target="tpu_custom_call" | custom-call | tf_op jit(solution)/shard_map/prepare/pallas_call | solution.py:451
  14.6 0.0 collective-permute-done.3.rim
  14.6 0.0 copy-start.6
  14.6 0.6 copy-done.6
  15.2 14.6 %forward_old.1 = (f32[4,1088,128]{2,1,0:T(8,128)}, f32[4,1024,128]{2,1,0:T(8,128)}, f32[4,1024,128]{2,1,0:T(8,128)}, f32[4,1024,128]{2,1,0:T(8,128)}, f32[4,1024...) custom-call(s32[152]{0:T(256)} %get-tuple-element.33.meta, bf16[128,4096]{1,0:T(8,128)(2,1)} %bitcast.20, ...), custom_call_target="tpu_custom_call" | custom-call | flops 57671680 | bytes 14680064 | tf_op jit(solution)/shard_map/forward_old/pallas_call | solution.py:475
  29.8 2.0 %collective-permute-start.5 = (f32[4,128,128]{2,1,0:T(8,128)}, f32[4,128,128]{2,1,0:T(8,128)S(1)}, u32[]{:S(2)}, u32[]{:S(2)}) collective-permute-start(f32[4,128,128]{2,1,0:T(8,128)} %get-tuple-element.40), channel_id=1, source_target_pairs={{0,4},{4,8},{8,12},{12,16},{16,20},{20,24},{24,28},{1,5},{5,9},{9,... | collective-permute-start | bytes 786440 | tf_op jit(solution)/shard_map/ppermute | solution.py:21
  31.8 0.0 collective-permute-done.1.rim
  31.9 0.0 copy-start.5
  31.9 0.0 collective-permute-done
  31.9 0.0 copy-start.2
  31.9 0.6 copy-done.5
  32.5 0.4 copy-done.2
  32.9 14.2 %forward_new.1 = (f32[4,1024,128]{2,1,0:T(8,128)}, f32[4,1024,128]{2,1,0:T(8,128)}, f32[4,1024,128]{2,1,0:T(8,128)}, f32[4,128,128]{2,1,0:T(8,128)}) custom-call(s32[152]{0:T(256)} %get-tuple-element.26.meta, bf16[128,4096]{1,0:T(8,128)(2,1)} %bitcast.22, bf16[8,4096]{1,0:T(8,128)(2,1)} %copy-done.5, f32[21,32,128]{2,1,0:T(8,128)} %bitcast.18, ...), custom_call_target="tpu_custom_call" | custom-call | flops 57671680 | bytes 8388608 | tf_op jit(solution)/shard_map/forward_new/pallas_call | solution.py:486
  47.0 2.2 %collective-permute-start.2 = (f32[4,128,128]{2,1,0:T(8,128)}, f32[4,128,128]{2,1,0:T(8,128)S(1)}, u32[]{:S(2)}, u32[]{:S(2)}) collective-permute-start(f32[4,128,128]{2,1,0:T(8,128)} %get-tuple-element.32), channel_id=1, source_target_pairs={{0,4},{4,8},{8,12},{12,16},{16,20},{20,24},{24,28},{1,5},{5,9},{9,... | collective-permute-start | bytes 786440 | tf_op jit(solution)/shard_map/ppermute | solution.py:21
  49.3 0.0 collective-permute-done.5.state
  49.3 0.0 copy-start.4
  49.3 0.0 collective-permute-done.4
  49.3 0.0 copy-start
  49.3 6.6 %collective-permute-done.2.state.after = f32[4,128,128]{2,1,0:T(8,128)S(1)} collective-permute-done((f32[4,128,128]{2,1,0:T(8,128)}, f32[4,128,128]{2,1,0:T(8,128)S(1)}, u32[]{:S(2)}, u32[]{:S(2)}) %collective-permute-start.2) | collective-permute-done | bytes 262176 | tf_op jit(solution)/shard_map/ppermute | solution.py:21
  55.9 0.0 copy-start.1
  55.9 0.0 copy-done.4
  55.9 0.0 copy-done
  55.9 0.7 copy-done.1
  56.6 11.7 %backward_main.1 = (f32[4,1024,128]{2,1,0:T(8,128)}, f32[4,1024,128]{2,1,0:T(8,128)}, f32[4,1024,128]{2,1,0:T(8,128)}, f32[4,320,128]{2,1,0:T(8,128)}, f32[4,128,128]{2,1,0:T(8,128)}) custom-call(s32[152]{0:T(256)} %get-tuple-element.33.meta, bf16[128,4096]{1,0:T(8,128)(2,1)} %bitcast.21, f32[4,1024,128]{2,1,0:T(8,128)} %get-tuple-element.38.qs, ...), custom_call_target="tpu_custom_call" | custom-call | flops 62914560 | bytes 16777216 | tf_op jit(solution)/shard_map/backward_main/pallas_call | solution.py:498
  68.3 1.3 collective-permute-start.6
  69.6 4.9 %mixed.1.after = bf16[128,4096]{1,0:T(8,128)(2,1)} custom-call(s32[152]{0:T(256)} %get-tuple-element.26.meta, f32[4,1024,128]{2,1,0:T(8,128)} %get-tuple-element.29.qs, f32[4,1024,128]{2,1,0:T(8,128)} %get-tuple-element.30.gs, f32[4,1024,128]{2,1,0:T(8,128)} %get-tuple-element.31.longs, f32[4,128,128]{2,1,0:T(8,128)} %copy-done.1, ...), custom_call_target="tpu_custom_call" | custom-call | flops 15728640 | bytes 8388608 | tf_op jit(solution)/shard_map/mixed/pallas_call | solution.py:523
  74.5 13.9 %collective-permute-done.6.turn = f32[4,320,128]{2,1,0:T(8,128)S(1)} collective-permute-done((f32[4,320,128]{2,1,0:T(8,128)}, f32[4,320,128]{2,1,0:T(8,128)S(1)}, u32[]{:S(2)}, u32[]{:S(2)}) %collective-permute-start.6) | collective-permute-done | bytes 655392 | tf_op jit(solution)/shard_map/ppermute | solution.py:21
  88.3 0.0 copy-start.3
  88.3 0.9 copy-done.3
  89.2 18.3 %finish.1 = (bf16[128,4096]{1,0:T(8,128)(2,1)}, f32[22,32,128]{2,1,0:T(8,128)}) custom-call(s32[152]{0:T(256)} %get-tuple-element.33.meta, f32[4,1088,128]{2,1,0:T(8,128)} %get-tuple-element.34.xs, f32[4,1024,128]{2,1,0:T(8,128)} %get-tuple-element.35.ks, f32[4,1024,128]{2,1,0:T(8,128)} %get-tuple-element.36.vs, f32[4,1024,128]{2,1,0:T(8,128)} %get-tuple-element.37.gs, ...), custom_call_target="tpu_custom_call" | custom-call | flops 78643200 | bytes 16777216 | tf_op jit(solution)/shard_map/finish/pallas_call | solution.py:535
  107.5 24.2 %window_sum.1 = f32[88,8,128]{2,1,0:T(8,128)} custom-call(f32[88,8,128]{2,1,0:T(8,128)} %bitcast.25), custom_call_target="tpu_custom_call" | custom-call | tf_op jit(solution)/shard_map/window_sum/pallas_call | solution.py:552
  131.7 0.7 slice.18
  132.4 1.7 %slice.19 = f32[84,8,128]{2,1,0:T(8,128)} slice(f32[88,8,128]{2,1,0:T(8,128)} %window_sum.1), slice={[0:84], [0:8], [0:128]} | slice | bytes 688128 | tf_op jit(solution)/shard_map/slice | solution.py:562
  134.1 0.2 reshape.16
  134.3 0.1 copy.13
  134.4 0.7 copy.14
Async XLA Ops:
  0.6 31.2 %collective-permute-start = (bf16[1,128,4096]{2,1,0:T(8,128)(2,1)}, bf16[1,128,4096]{2,1,0:T(8,128)(2,1)S(1)}, u32[]{:S(2)}, u32[]{:S(2)}) collective-permute-start(bf16[1,128,4096]{2,1,0:T(8,128)(2,1)} %param.7), channel_id=1, source_target_pairs={{0,1},{1,2},{2,3},{3,0},{4,5},{5,6},{6,7},{7,4},{8,9},{9,10},{10,1... | collective-permute-start | bytes 3145736 | tf_op jit(solution)/shard_map/ppermute | solution.py:26
  2.0 12.6 %collective-permute-start.3 = (bf16[8,4096]{1,0:T(8,128)(2,1)S(1)}, bf16[8,4096]{1,0:T(8,128)(2,1)S(1)}, u32[]{:S(2)}, u32[]{:S(2)}) collective-permute-start(bf16[8,4096]{1,0:T(8,128)(2,1)S(1)} %slice_bitcast_fusion), channel_id=1, source_target_pairs={{0,4},{4,8},{8,12},{12,16},{16,20},{20,24},{24,28},{1,5},{5,9},{9,... | collective-permute-start | bytes 196616 | tf_op jit(solution)/shard_map/ppermute | solution.py:21
  6.4 42.9 %collective-permute-start.4 = (bf16[1,128,4096]{2,1,0:T(8,128)(2,1)}, bf16[1,128,4096]{2,1,0:T(8,128)(2,1)S(1)}, u32[]{:S(2)}, u32[]{:S(2)}) collective-permute-start(bf16[1,128,4096]{2,1,0:T(8,128)(2,1)} %param.9), channel_id=1, source_target_pairs={{0,3},{1,0},{2,1},{3,2},{4,7},{5,4},{6,5},{7,6},{8,11},{9,8},{10,9... | collective-permute-start | bytes 3145736 | tf_op jit(solution)/shard_map/ppermute | solution.py:26
  8.8 23.1 %collective-permute-start.1 = (bf16[8,4096]{1,0:T(8,128)(2,1)S(1)}, bf16[8,4096]{1,0:T(8,128)(2,1)S(1)}, u32[]{:S(2)}, u32[]{:S(2)}) collective-permute-start(bf16[8,4096]{1,0:T(8,128)(2,1)S(1)} %slice_bitcast_fusion.1), channel_id=1, source_target_pairs={{0,5},{1,6},{2,7},{3,4},{4,9},{5,10},{6,11},{7,8},{8,13},{9,14},{1... | collective-permute-start | bytes 196616 | tf_op jit(solution)/shard_map/ppermute | solution.py:438
  14.6 0.6 copy-start.6
  29.8 19.4 %collective-permute-start.5 = (f32[4,128,128]{2,1,0:T(8,128)}, f32[4,128,128]{2,1,0:T(8,128)S(1)}, u32[]{:S(2)}, u32[]{:S(2)}) collective-permute-start(f32[4,128,128]{2,1,0:T(8,128)} %get-tuple-element.40), channel_id=1, source_target_pairs={{0,4},{4,8},{8,12},{12,16},{16,20},{20,24},{24,28},{1,5},{5,9},{9,... | collective-permute-start | bytes 786440 | tf_op jit(solution)/shard_map/ppermute | solution.py:21
  31.9 0.6 copy-start.5
  31.9 1.0 copy-start.2
  47.0 8.9 %collective-permute-start.2 = (f32[4,128,128]{2,1,0:T(8,128)}, f32[4,128,128]{2,1,0:T(8,128)S(1)}, u32[]{:S(2)}, u32[]{:S(2)}) collective-permute-start(f32[4,128,128]{2,1,0:T(8,128)} %get-tuple-element.32), channel_id=1, source_target_pairs={{0,4},{4,8},{8,12},{12,16},{16,20},{20,24},{24,28},{1,5},{5,9},{9,... | collective-permute-start | bytes 786440 | tf_op jit(solution)/shard_map/ppermute | solution.py:21
  49.3 6.7 %copy-start.4 = (f32[4,128,128]{2,1,0:T(8,128)}, f32[4,128,128]{2,1,0:T(8,128)S(1)}, u32[]{:S(2)}) copy-start(f32[4,128,128]{2,1,0:T(8,128)S(1)} %collective-permute-done.5.state) | copy-start | bytes 786436
  49.3 6.6 %copy-start = (bf16[1,128,4096]{2,1,0:T(8,128)(2,1)}, bf16[1,128,4096]{2,1,0:T(8,128)(2,1)S(1)}, u32[]{:S(2)}) copy-start(bf16[1,128,4096]{2,1,0:T(8,128)(2,1)S(1)} %collective-permute-done.4) | copy-start | bytes 3145732
  55.9 0.7 copy-start.1
  68.3 20.1 %collective-permute-start.6 = (f32[4,320,128]{2,1,0:T(8,128)}, f32[4,320,128]{2,1,0:T(8,128)S(1)}, u32[]{:S(2)}, u32[]{:S(2)}) collective-permute-start(f32[4,320,128]{2,1,0:T(8,128)} %get-tuple-element.44), channel_id=1, source_target_pairs={{4,0},{8,4},{12,8},{16,12},{20,16},{24,20},{28,24},{5,1},{9,5},{13... | collective-permute-start | bytes 1966088 | tf_op jit(solution)/shard_map/ppermute | solution.py:21
  88.3 0.9 copy-start.3

commit v4 on v3

--- a/solution.py
+++ b/solution.py
@@ -8,7 +8,7 @@
 
 
 F32 = jnp.float32
-SHIFT = 2
+SHIFT = 3
 UNROLL = 1 << SHIFT
 LANES = 128
 SUB = 8
@@ -124,8 +124,8 @@
 
     def feats(g, window):
         window = list(window)
-        for u in range(2):
-            t = g * 2 + u
+        for u in range(4):
+            t = g * 4 + u
             keep = meta[HEAD + t].astype(F32)
             now = at(xs, t + 8)
             seen = [now] + [w * keep for w in window]
@@ -141,7 +141,7 @@
             window = seen[:-1]
         return tuple(window)
 
-    lax.fori_loop(0, rows // 2, feats, window)
+    lax.fori_loop(0, rows // 4, feats, window)
     init = tuple(jnp.zeros((SUB, LANES), F32) for _ in range(modes))
     states = scan_forward(
         meta, gs, dtab, resid, meta[1], rows // UNROLL, init, lambda t, y: put(longs, t, y)
@@ -195,11 +195,12 @@
     for m in range(modes):
         put(turn, m, states[m])
         put(sums, m, totals[m])
-    for t in range(8):
+    halo = (turn.shape[0] // SUB - modes) // 3
+    for t in range(halo):
         value = at(dg, t)
         put(turn, modes + t, at(dq, t))
-        put(turn, modes + 8 + t, value * at(vs, t))
-        put(turn, modes + 16 + t, value * at(ks, t))
+        put(turn, modes + halo + t, value * at(vs, t))
+        put(turn, modes + 2 * halo + t, value * at(ks, t))
 
 
 def finish_kernel(
@@ -245,13 +246,13 @@
 
     pending = tuple(jnp.zeros((SUB, LANES), F32) for _ in range(taps_count - 1))
     for r in reversed(range(taps_count - 1)):
-        grads = [at(turn, modes + i * 8 + r) for i in range(3)]
+        grads = [at(turn, modes + i * (taps_count - 1) + r) for i in range(3)]
         _, pending = spread(pending, grads, meta[HEAD + rows + r].astype(F32))
 
     def descend(i, pending):
-        g = rows // 2 - 1 - i
-        for u in reversed(range(2)):
-            t = g * 2 + u
+        g = rows // 4 - 1 - i
+        for u in reversed(range(4)):
+            t = g * 4 + u
             gated = at(dks, t)
             dk = gated * at(vs, t)
             dv = gated * at(ks, t)
@@ -261,7 +262,7 @@
             put(backs, t, done)
         return pending
 
-    lax.fori_loop(0, rows // 2, descend, pending)
+    lax.fori_loop(0, rows // 4, descend, pending)
     gather_rows(backs, out, rows)
     age = meta[5]
     window = tuple(
@@ -271,8 +272,8 @@
 
     def ascend(g, carry):
         window, acc = list(carry[0]), list(carry[1])
-        for u in range(2):
-            t = g * 2 + u
+        for u in range(4):
+            t = g * 4 + u
             keep = meta[HEAD + t].astype(F32)
             seen = [at(xs, t + 8)] + [w * keep for w in window]
             grads = [at(dq, t), at(dks, t), at(dvs, t)]
@@ -284,7 +285,7 @@
             window = seen[:-1]
         return tuple(window), tuple(acc)
 
-    _, acc = lax.fori_loop(0, rows // 2, ascend, (window, zeros))
+    _, acc = lax.fori_loop(0, rows // 4, ascend, (window, zeros))
     for n in range(3 * taps_count):
         tap_out[n] = acc[n]
 
@@ -499,8 +500,8 @@
         functools.partial(backward_kernel, rows, modes),
         grid=(blocks,),
         in_specs=[smem, tokens] + [major(rows)] * 5 + [major(modes)] + tail[1:] + [anywhere],
-        out_specs=[major(rows)] * 3 + [major(modes + 24), major(modes)],
-        out_shape=[shaped(rows)] * 3 + [shaped(modes + 24), shaped(modes)],
+        out_specs=[major(rows)] * 3 + [major(modes + 3 * (taps_count - 1)), major(modes)],
+        out_shape=[shaped(rows)] * 3 + [shaped(modes + 3 * (taps_count - 1)), shaped(modes)],
         scratch_shapes=[scratch(rows)],
         cost_estimate=cost(120, 8),
         name="backward_main",
@@ -512,9 +513,9 @@
         rim = turn[:, modes * SUB :]
         spread = (blocks, modes, SUB, LANES)
         extra = jnp.stack(
-            [jnp.sum((resid * later * decay ** (rows - r)).reshape(spread), axis=1) for r in range(8)], axis=1
-        ).reshape(blocks, 8 * SUB, LANES) * through_old
-        head = 8 * SUB
+            [jnp.sum((resid * later * decay ** (rows - r)).reshape(spread), axis=1) for r in range(taps_count - 1)], axis=1
+        ).reshape(blocks, (taps_count - 1) * SUB, LANES) * through_old
+        head = (taps_count - 1) * SUB
         rim = rim + jnp.concatenate(
             [jnp.zeros_like(extra), extra * vs[:, :head], extra * ks[:, :head]], axis=1
         )
@@ -535,7 +536,7 @@
     back, partial = pl.pallas_call(
         functools.partial(finish_kernel, rows, modes, taps_count, group),
         grid=(blocks,),
-        in_specs=[smem, major(rows + 8)] + [major(rows)] * 6 + [major(modes + 24), major(modes)] + tail + [anywhere],
+        in_specs=[smem, major(rows + 8)] + [major(rows)] * 6 + [major(modes + 3 * (taps_count - 1)), major(modes)] + tail + [anywhere],
         out_specs=[tokens, pl.BlockSpec((slots, SUB, LANES), lambda b: (0, b, 0))],
         out_shape=[wide, jax.ShapeDtypeStruct((slots, blocks * SUB, LANES), F32)],
         scratch_shapes=[scratch(rows)] * 3,

time: 136 us -> 126 us (0.926)
  Pallas kernels: 90.6 us -> 83 us
  waiting for transfers between devices: 20.5 us -> 18.3 us
    pallas_call x2, Pallas kernels: 28.8 us -> 24.9 us  [on_device(): pl.pallas_call(functools.partial(forward_kernel, rows, modes, taps_count,...]
    pallas_call x1, Pallas kernels: 18.3 us -> 15.8 us  [on_device(): pl.pallas_call(functools.partial(finish_kernel, rows, modes, taps_count,...]
    ppermute x4, waiting for transfers between devices: 20.5 us -> 18.3 us  [from_behind(): lax.ppermute(value, axis, [(source, source + steps) for source in range(i...]
  transfers between devices with their start and end apart: 7 -> 7, of which waited for: 2 -> 2; matrix products, arithmetic and copies ran while one was open for 1% -> 1% of each run, Pallas kernels for 27% -> 26%
where the time goes in v4:
time: 126 us
  Pallas kernels  83 us (66%)
  waiting for transfers between devices  18.3 us (15%)
  starting transfers between devices  15.4 us (12%)
  local copies, waits for them, and re-layouts  8.21 us (7%)
    pallas_call x2, Pallas kernels, on_device(): pl.pallas_call(functools.partial(forward_kernel, rows, modes, taps_count,...  24.9 us
    pallas_call x1, Pallas kernels, on_device(): pl.pallas_call(functools.partial(sum_kernel, ctx_size, chunk), in_specs=[...  23.3 us
    ppermute x4, waiting for transfers between devices, from_behind(): lax.ppermute(value, axis, [(source, source + steps) for source in range(i...  18.3 us
    pallas_call x1, Pallas kernels, on_device(): pl.pallas_call(functools.partial(finish_kernel, rows, modes, taps_count,...  15.8 us
    pallas_call x1, Pallas kernels, on_device(): pl.pallas_call(functools.partial(backward_kernel, rows, modes), grid=(blo...  11.3 us
    ppermute x4, starting transfers between devices, from_behind(): lax.ppermute(value, axis, [(source, source + steps) for source in range(i...  10.4 us
    pallas_call x1, Pallas kernels, on_device(): pl.pallas_call(functools.partial(mixed_kernel, rows, modes), grid=(blocks...  4.89 us
    unnamed x15, local copies, waits for them, and re-layouts  3.81 us
  transfers between devices with their start and end apart: 7, of which 2 were waited for; matrix products, arithmetic and copies ran while one was open for 1% of the time, Pallas kernels for 26%

profile of v4, /device:TPU:0, one launch (start us, length us, event | category | flops | bytes accessed | tf_op | source)
XLA Modules:
  0.0 125.6 jit_solution(5032321611374863729)
XLA Ops:
  0.6 0.5 collective-permute-start
  1.2 0.8 slice_bitcast_fusion
  2.0 4.4 %collective-permute-start.3 = (bf16[8,4096]{1,0:T(8,128)(2,1)S(1)}, bf16[8,4096]{1,0:T(8,128)(2,1)S(1)}, u32[]{:S(2)}, u32[]{:S(2)}) collective-permute-start(bf16[8,4096]{1,0:T(8,128)(2,1)S(1)} %slice_bitcast_fusion), channel_id=1, source_target_pairs={{0,4},{4,8},{8,12},{12,16},{16,20},{20,24},{24,28},{1,5},{5,9},{9,... | collective-permute-start | bytes 196616 | tf_op jit(solution)/shard_map/ppermute | solution.py:21
  6.4 1.5 %collective-permute-start.4 = (bf16[1,128,4096]{2,1,0:T(8,128)(2,1)}, bf16[1,128,4096]{2,1,0:T(8,128)(2,1)S(1)}, u32[]{:S(2)}, u32[]{:S(2)}) collective-permute-start(bf16[1,128,4096]{2,1,0:T(8,128)(2,1)} %param.9), channel_id=1, source_target_pairs={{0,3},{1,0},{2,1},{3,2},{4,7},{5,4},{6,5},{7,6},{8,11},{9,8},{10,9... | collective-permute-start | bytes 3145736 | tf_op jit(solution)/shard_map/ppermute | solution.py:26
  7.9 0.8 slice_bitcast_fusion.1
  8.8 3.0 %collective-permute-start.1 = (bf16[8,4096]{1,0:T(8,128)(2,1)S(1)}, bf16[8,4096]{1,0:T(8,128)(2,1)S(1)}, u32[]{:S(2)}, u32[]{:S(2)}) collective-permute-start(bf16[8,4096]{1,0:T(8,128)(2,1)S(1)} %slice_bitcast_fusion.1), channel_id=1, source_target_pairs={{0,5},{1,6},{2,7},{3,4},{4,9},{5,10},{6,11},{7,8},{8,13},{9,14},{1... | collective-permute-start | bytes 196616 | tf_op jit(solution)/shard_map/ppermute | solution.py:439
  11.7 2.8 %prepare.1 = (s32[152]{0:T(256)}, s32[152]{0:T(256)}, f32[4,256,128]{2,1,0:T(8,128)}, f32[4,128,128]{2,1,0:T(8,128)}) custom-call(s32[2,24]{1,0:T(2,128)} %lengths.1, f32[16,256]{1,0:T(8,128)} %bitcast.27, f32[16,256]{1,0:T(8,128)} %bitcast.28), custom_call_target="tpu_custom_call" | custom-call | tf_op jit(solution)/shard_map/prepare/pallas_call | solution.py:452
  14.6 0.0 collective-permute-done.3.rim
  14.6 0.0 copy-start.6
  14.6 0.6 copy-done.6
  15.2 12.7 %forward_old.1 = (f32[4,1088,128]{2,1,0:T(8,128)}, f32[4,1024,128]{2,1,0:T(8,128)}, f32[4,1024,128]{2,1,0:T(8,128)}, f32[4,1024,128]{2,1,0:T(8,128)}, f32[4,1024...) custom-call(s32[152]{0:T(256)} %get-tuple-element.33.meta, bf16[128,4096]{1,0:T(8,128)(2,1)} %bitcast.20, ...), custom_call_target="tpu_custom_call" | custom-call | flops 57671680 | bytes 14680064 | tf_op jit(solution)/shard_map/forward_old/pallas_call | solution.py:476
  28.0 2.2 %collective-permute-start.5 = (f32[4,128,128]{2,1,0:T(8,128)}, f32[4,128,128]{2,1,0:T(8,128)S(1)}, u32[]{:S(2)}, u32[]{:S(2)}) collective-permute-start(f32[4,128,128]{2,1,0:T(8,128)} %get-tuple-element.40), channel_id=1, source_target_pairs={{0,4},{4,8},{8,12},{12,16},{16,20},{20,24},{24,28},{1,5},{5,9},{9,... | collective-permute-start | bytes 786440 | tf_op jit(solution)/shard_map/ppermute | solution.py:21
  30.1 0.0 collective-permute-done.1.rim
  30.1 0.0 copy-start.5
  30.1 0.0 collective-permute-done
  30.2 0.0 copy-start.2
  30.2 0.6 copy-done.5
  30.8 0.4 copy-done.2
  31.1 12.2 %forward_new.1 = (f32[4,1024,128]{2,1,0:T(8,128)}, f32[4,1024,128]{2,1,0:T(8,128)}, f32[4,1024,128]{2,1,0:T(8,128)}, f32[4,128,128]{2,1,0:T(8,128)}) custom-call(s32[152]{0:T(256)} %get-tuple-element.26.meta, bf16[128,4096]{1,0:T(8,128)(2,1)} %bitcast.22, bf16[8,4096]{1,0:T(8,128)(2,1)} %copy-done.5, f32[21,32,128]{2,1,0:T(8,128)} %bitcast.18, ...), custom_call_target="tpu_custom_call" | custom-call | flops 57671680 | bytes 8388608 | tf_op jit(solution)/shard_map/forward_new/pallas_call | solution.py:487
  43.3 2.5 %collective-permute-start.2 = (f32[4,128,128]{2,1,0:T(8,128)}, f32[4,128,128]{2,1,0:T(8,128)S(1)}, u32[]{:S(2)}, u32[]{:S(2)}) collective-permute-start(f32[4,128,128]{2,1,0:T(8,128)} %get-tuple-element.32), channel_id=1, source_target_pairs={{0,4},{4,8},{8,12},{12,16},{16,20},{20,24},{24,28},{1,5},{5,9},{9,... | collective-permute-start | bytes 786440 | tf_op jit(solution)/shard_map/ppermute | solution.py:21
  45.8 0.0 collective-permute-done.5.state
  45.8 0.0 copy-start.4
  45.9 0.0 collective-permute-done.4
  45.9 0.0 copy-start
  45.9 6.6 %collective-permute-done.2.state.after = f32[4,128,128]{2,1,0:T(8,128)S(1)} collective-permute-done((f32[4,128,128]{2,1,0:T(8,128)}, f32[4,128,128]{2,1,0:T(8,128)S(1)}, u32[]{:S(2)}, u32[]{:S(2)}) %collective-permute-start.2) | collective-permute-done | bytes 262176 | tf_op jit(solution)/shard_map/ppermute | solution.py:21
  52.5 0.0 copy-start.1
  52.5 0.0 copy-done.4
  52.5 0.0 copy-done
  52.5 0.7 copy-done.1
  53.2 11.3 %backward_main.1 = (f32[4,1024,128]{2,1,0:T(8,128)}, f32[4,1024,128]{2,1,0:T(8,128)}, f32[4,1024,128]{2,1,0:T(8,128)}, f32[4,272,128]{2,1,0:T(8,128)}, f32[4,128,128]{2,1,0:T(8,128)}) custom-call(s32[152]{0:T(256)} %get-tuple-element.33.meta, bf16[128,4096]{1,0:T(8,128)(2,1)} %bitcast.21, f32[4,1024,128]{2,1,0:T(8,128)} %get-tuple-element.38.qs, ...), custom_call_target="tpu_custom_call" | custom-call | flops 62914560 | bytes 16777216 | tf_op jit(solution)/shard_map/backward_main/pallas_call | solution.py:499
  64.5 1.3 %collective-permute-start.6 = (f32[4,272,128]{2,1,0:T(8,128)}, f32[4,272,128]{2,1,0:T(8,128)S(1)}, u32[]{:S(2)}, u32[]{:S(2)}) collective-permute-start(f32[4,272,128]{2,1,0:T(8,128)} %get-tuple-element.44), channel_id=1, source_target_pairs={{4,0},{8,4},{12,8},{16,12},{20,16},{24,20},{28,24},{5,1},{9,5},{13... | collective-permute-start | bytes 1671176 | tf_op jit(solution)/shard_map/ppermute | solution.py:21
  65.8 4.9 %mixed.1.after = bf16[128,4096]{1,0:T(8,128)(2,1)} custom-call(s32[152]{0:T(256)} %get-tuple-element.26.meta, f32[4,1024,128]{2,1,0:T(8,128)} %get-tuple-element.29.qs, f32[4,1024,128]{2,1,0:T(8,128)} %get-tuple-element.30.gs, f32[4,1024,128]{2,1,0:T(8,128)} %get-tuple-element.31.longs, f32[4,128,128]{2,1,0:T(8,128)} %copy-done.1, ...), custom_call_target="tpu_custom_call" | custom-call | flops 15728640 | bytes 8388608 | tf_op jit(solution)/shard_map/mixed/pallas_call | solution.py:524
  70.7 11.7 %collective-permute-done.6.turn = f32[4,272,128]{2,1,0:T(8,128)S(1)} collective-permute-done((f32[4,272,128]{2,1,0:T(8,128)}, f32[4,272,128]{2,1,0:T(8,128)S(1)}, u32[]{:S(2)}, u32[]{:S(2)}) %collective-permute-start.6) | collective-permute-done | bytes 557088 | tf_op jit(solution)/shard_map/ppermute | solution.py:21
  82.3 0.0 copy-start.3
  82.3 0.8 copy-done.3
  83.1 15.8 %finish.1 = (bf16[128,4096]{1,0:T(8,128)(2,1)}, f32[22,32,128]{2,1,0:T(8,128)}) custom-call(s32[152]{0:T(256)} %get-tuple-element.33.meta, f32[4,1088,128]{2,1,0:T(8,128)} %get-tuple-element.34.xs, f32[4,1024,128]{2,1,0:T(8,128)} %get-tuple-element.35.ks, f32[4,1024,128]{2,1,0:T(8,128)} %get-tuple-element.36.vs, f32[4,1024,128]{2,1,0:T(8,128)} %get-tuple-element.37.gs, ...), custom_call_target="tpu_custom_call" | custom-call | flops 78643200 | bytes 16777216 | tf_op jit(solution)/shard_map/finish/pallas_call | solution.py:536
  98.9 23.3 %window_sum.1 = f32[88,8,128]{2,1,0:T(8,128)} custom-call(f32[88,8,128]{2,1,0:T(8,128)} %bitcast.25), custom_call_target="tpu_custom_call" | custom-call | tf_op jit(solution)/shard_map/window_sum/pallas_call | solution.py:553
  122.2 0.7 slice.18
  122.9 1.7 %slice.19 = f32[84,8,128]{2,1,0:T(8,128)} slice(f32[88,8,128]{2,1,0:T(8,128)} %window_sum.1), slice={[0:84], [0:8], [0:128]} | slice | bytes 688128 | tf_op jit(solution)/shard_map/slice | solution.py:563
  124.7 0.2 reshape.16
  124.8 0.1 copy.13
  124.9 0.7 copy.14
Async XLA Ops:
  0.6 29.5 %collective-permute-start = (bf16[1,128,4096]{2,1,0:T(8,128)(2,1)}, bf16[1,128,4096]{2,1,0:T(8,128)(2,1)S(1)}, u32[]{:S(2)}, u32[]{:S(2)}) collective-permute-start(bf16[1,128,4096]{2,1,0:T(8,128)(2,1)} %param.7), channel_id=1, source_target_pairs={{0,1},{1,2},{2,3},{3,0},{4,5},{5,6},{6,7},{7,4},{8,9},{9,10},{10,1... | collective-permute-start | bytes 3145736 | tf_op jit(solution)/shard_map/ppermute | solution.py:26
  2.0 12.6 %collective-permute-start.3 = (bf16[8,4096]{1,0:T(8,128)(2,1)S(1)}, bf16[8,4096]{1,0:T(8,128)(2,1)S(1)}, u32[]{:S(2)}, u32[]{:S(2)}) collective-permute-start(bf16[8,4096]{1,0:T(8,128)(2,1)S(1)} %slice_bitcast_fusion), channel_id=1, source_target_pairs={{0,4},{4,8},{8,12},{12,16},{16,20},{20,24},{24,28},{1,5},{5,9},{9,... | collective-permute-start | bytes 196616 | tf_op jit(solution)/shard_map/ppermute | solution.py:21
  6.4 39.4 %collective-permute-start.4 = (bf16[1,128,4096]{2,1,0:T(8,128)(2,1)}, bf16[1,128,4096]{2,1,0:T(8,128)(2,1)S(1)}, u32[]{:S(2)}, u32[]{:S(2)}) collective-permute-start(bf16[1,128,4096]{2,1,0:T(8,128)(2,1)} %param.9), channel_id=1, source_target_pairs={{0,3},{1,0},{2,1},{3,2},{4,7},{5,4},{6,5},{7,6},{8,11},{9,8},{10,9... | collective-permute-start | bytes 3145736 | tf_op jit(solution)/shard_map/ppermute | solution.py:26
  8.8 21.4 %collective-permute-start.1 = (bf16[8,4096]{1,0:T(8,128)(2,1)S(1)}, bf16[8,4096]{1,0:T(8,128)(2,1)S(1)}, u32[]{:S(2)}, u32[]{:S(2)}) collective-permute-start(bf16[8,4096]{1,0:T(8,128)(2,1)S(1)} %slice_bitcast_fusion.1), channel_id=1, source_target_pairs={{0,5},{1,6},{2,7},{3,4},{4,9},{5,10},{6,11},{7,8},{8,13},{9,14},{1... | collective-permute-start | bytes 196616 | tf_op jit(solution)/shard_map/ppermute | solution.py:439
  14.6 0.6 copy-start.6
  28.0 17.9 %collective-permute-start.5 = (f32[4,128,128]{2,1,0:T(8,128)}, f32[4,128,128]{2,1,0:T(8,128)S(1)}, u32[]{:S(2)}, u32[]{:S(2)}) collective-permute-start(f32[4,128,128]{2,1,0:T(8,128)} %get-tuple-element.40), channel_id=1, source_target_pairs={{0,4},{4,8},{8,12},{12,16},{16,20},{20,24},{24,28},{1,5},{5,9},{9,... | collective-permute-start | bytes 786440 | tf_op jit(solution)/shard_map/ppermute | solution.py:21
  30.1 0.6 copy-start.5
  30.2 1.0 copy-start.2
  43.3 9.2 %collective-permute-start.2 = (f32[4,128,128]{2,1,0:T(8,128)}, f32[4,128,128]{2,1,0:T(8,128)S(1)}, u32[]{:S(2)}, u32[]{:S(2)}) collective-permute-start(f32[4,128,128]{2,1,0:T(8,128)} %get-tuple-element.32), channel_id=1, source_target_pairs={{0,4},{4,8},{8,12},{12,16},{16,20},{20,24},{24,28},{1,5},{5,9},{9,... | collective-permute-start | bytes 786440 | tf_op jit(solution)/shard_map/ppermute | solution.py:21
  45.8 6.7 %copy-start.4 = (f32[4,128,128]{2,1,0:T(8,128)}, f32[4,128,128]{2,1,0:T(8,128)S(1)}, u32[]{:S(2)}) copy-start(f32[4,128,128]{2,1,0:T(8,128)S(1)} %collective-permute-done.5.state) | copy-start | bytes 786436
  45.9 6.6 %copy-start = (bf16[1,128,4096]{2,1,0:T(8,128)(2,1)}, bf16[1,128,4096]{2,1,0:T(8,128)(2,1)S(1)}, u32[]{:S(2)}) copy-start(bf16[1,128,4096]{2,1,0:T(8,128)(2,1)S(1)} %collective-permute-done.4) | copy-start | bytes 3145732
  52.5 0.7 copy-start.1
  64.5 17.8 %collective-permute-start.6 = (f32[4,272,128]{2,1,0:T(8,128)}, f32[4,272,128]{2,1,0:T(8,128)S(1)}, u32[]{:S(2)}, u32[]{:S(2)}) collective-permute-start(f32[4,272,128]{2,1,0:T(8,128)} %get-tuple-element.44), channel_id=1, source_target_pairs={{4,0},{8,4},{12,8},{16,12},{20,16},{24,20},{28,24},{5,1},{9,5},{13... | collective-permute-start | bytes 1671176 | tf_op jit(solution)/shard_map/ppermute | solution.py:21
  82.3 0.8 copy-start.3
